TPU v7x, 128 devices: a whole 4x4x4 slice. The times are simulated.
128 devices in a mesh: ia: 16 (over z, x_lo, core), ka: 8 (over y, x_hi).
Axes of the slice: x: 4 (x_hi: 2, x_lo: 2; x = x_hi * 2 + x_lo), y: 4, z: 4, core: 2. Of those that a mesh axis runs over, the one named last changes fastest.
Arguments:
- amplitudes: float32 [16, 16, 1024, 1024], P('ia', 'ka'), may hold values from -3 to 3
- integrals: bfloat16 [16, 2, 16, 1024, 1024], P('ia', None, 'ka'), may hold values from -0.046875 to 0.046875
- tile_mask: int32 [16, 2, 16, 8, 8], P('ia', None, 'ka'), may hold values from 0 to 1, as said below
- pair_list: int32 [16, 2], replicated, may hold values from 0 to 15, as said below
Outputs:
- residual: float32 [16, 2, 1024, 1024], P('ia', None, 'ka')
Inputs may be any that keep to these rules, and one draw needn't show every extreme that they name: `tile_mask`: 1 marks a filled 128 x 128 tile of an integral block, 0 an empty one. `pair_list`: row i names two different occupied indices, neither equal to i; j stands in row i exactly when i stands in row j.
All inputs are finite; a program needn't handle non-finite values.
Results may differ from a plain program's by a relative error of at most 0.0003.
Values sent between devices are 32-bit elements; how exact they have to be, the bound alone decides.
A program may use at most 192 MiB of HBM per device.

v0:
```python
import jax
import jax.numpy as jnp
from jax import lax
from jax.sharding import PartitionSpec as P


def expand_mask(tile_mask, tile_side):
    grown = jnp.repeat(jnp.repeat(tile_mask, tile_side, axis=-2), tile_side, axis=-1)
    return grown.astype(jnp.float32)


def mirror_direct(amplitudes):
    row_groups = lax.axis_size("ia")
    col_groups = lax.axis_size("ka")
    local_pairs = amplitudes.shape[1]
    virtuals = amplitudes.shape[3]
    slab_rows = virtuals // (row_groups * col_groups)
    spread = lax.all_to_all(amplitudes, ("ia", "ka"), split_axis=2, concat_axis=0, tiled=True)
    spread = spread.reshape(col_groups, local_pairs, col_groups, local_pairs, slab_rows, virtuals)
    routed = jnp.transpose(spread, (2, 3, 0, 1, 4, 5))
    routed = routed.reshape(row_groups * col_groups, local_pairs, slab_rows, virtuals)
    delivered = lax.all_to_all(routed, ("ia", "ka"), split_axis=0, concat_axis=2, tiled=True)
    return delivered.reshape(local_pairs, virtuals, virtuals)


def body(amplitudes, integrals, tile_mask, pair_list):
    mirrored = mirror_direct(amplitudes)
    mixed = 2.0 * amplitudes[0] - jnp.swapaxes(mirrored, 1, 2)
    tile_side = integrals.shape[-1] // tile_mask.shape[-1]
    masked = integrals[0].astype(jnp.float32) * expand_mask(tile_mask[0], tile_side)
    partial_value = jnp.einsum("kxy,skyz->sxz", mixed, masked, precision=lax.Precision.HIGHEST)
    own_rows = lax.psum_scatter(partial_value, "ka", scatter_dimension=1, tiled=True)
    columns = lax.all_to_all(own_rows, "ka", split_axis=2, concat_axis=1, tiled=True)
    flipped = jnp.swapaxes(columns, 1, 2)
    spread = lax.all_to_all(flipped, "ia", split_axis=1, concat_axis=0, tiled=True)
    occupied = pair_list.shape[0]
    owners = jnp.arange(occupied, dtype=jnp.int32)
    partner_slot = jnp.where(pair_list[pair_list, 0] == owners[:, None], 0, 1).astype(jnp.int32)
    source_row = pair_list * 2 + partner_slot
    routed = jnp.take(spread, source_row.reshape(-1), axis=0)
    routed = routed.reshape(occupied, 2, spread.shape[1], spread.shape[2])
    delivered = lax.all_to_all(routed, "ia", split_axis=0, concat_axis=2, tiled=True)
    return (own_rows + delivered[0])[None]


def solution(mesh):
    placed = (
        P("ia", "ka", None, None),
        P("ia", None, "ka", None, None),
        P("ia", None, "ka", None, None),
        P(),
    )
    return jax.shard_map(
        body, mesh=mesh, in_specs=placed, out_specs=P("ia", None, "ka", None), check_vma=False
    )
```

profile of v0, /device:TPU:1, one launch (start us, length us, event | category | flops | bytes accessed | tf_op | source)
XLA Modules:
  0.0 493.9 jit_solution(5589319293559345768)
XLA Ops:
  6.5 14.4 %copy.114 = f32[1,2,1024,1024]{3,1,0,2:T(2,128)S(1)} copy(f32[1,2,1024,1024]{3,2,1,0:T(8,128)} %param.4) | data formatting | bytes 16777216 | tf_op args[0]
  20.9 108.9 %all_to_all.81 = f32[1,2,1024,1024]{3,1,0,2:T(2,128)S(1)} all-to-all(f32[1,2,1024,1024]{3,1,0,2:T(2,128)S(1)} %copy.114), channel_id=1, replica_groups=mesh['ia'=16,'ka'=8] {'ia','ka'}, dimensions={2} | all-to-all | bytes 16777216 | tf_op jit(solution)/shard_map/all_to_all | solution.py:18
  129.9 2.7 copy.115
  132.6 4.1 copy.117
  136.6 5.7 %all-to-all-start.1 = ((f32[128,2,8,1024]{3,2,1,0:T(8,128)}), f32[128,2,8,1024]{3,2,1,0:T(8,128)}, u32[]{:S(2)}, u32[]{:S(2)}) async-start(f32[128,2,8,1024]{3,2,1,0:T(8,128)} %bitcast.94), calls=%async_computation.1 | async-start | bytes 16777216 | tf_op jit(solution)/shard_map/all_to_all | solution.py:22
  142.4 8.7 %copy.113 = f32[1,2,1024,1024]{2,3,1,0:T(8,128)} copy(f32[1,2,1024,1024]{3,2,1,0:T(8,128)} %param.4) | data formatting | bytes 16777216 | tf_op args[0]
  151.1 0.1 broadcast_in_dim.30
  151.2 6.9 %broadcast_in_dim.31 = f32[2,2,1024,8,128]{4,3,2,1,0:T(8,128)} broadcast(f32[2,2,1024,8]{3,2,1,0:T(8,128)S(1)} %bitcast.96), dimensions={0,1,2,3} | broadcast | bytes 16908288 | tf_op jit(solution)/shard_map/broadcast_in_dim | solution.py:8
  158.1 18.0 %convert_element_type.25 = f32[2,2,1024,1024]{3,2,1,0:T(8,128)} reshape(f32[2,2,1024,8,128]{4,3,2,1,0:T(8,128)} %broadcast_in_dim.31) | data formatting | bytes 33554432 | tf_op jit(solution)/shard_map/convert_element_type | solution.py:9
  176.1 67.6 %all-to-all-done.1 = f32[128,2,8,1024]{3,2,1,0:T(8,128)} async-done(((f32[128,2,8,1024]{3,2,1,0:T(8,128)}), f32[128,2,8,1024]{3,2,1,0:T(8,128)}, u32[]{:S(2)}, u32[]{:S(2)}) %all-to-all-start.1) | async-done | bytes 8388640 | tf_op jit(solution)/shard_map/all_to_all | solution.py:22
  243.8 62.6 %fusion.8 = f32[2,1024,1024]{1,2,0:T(8,128)} fusion(f32[1,2,1024,1024]{2,3,1,0:T(8,128)} %copy.113, f32[2,2,1024,1024]{3,2,1,0:T(8,128)} %convert_element_type.25, bf16[1,2,2,1024,1024]{4,3,2,1,0:T(8,128)(2,1)} %param.5, f32[128,2,8,1024]{3,2,1,0:T(8,128)} %all-to-all-done.1), kind=kOutput, calls=%fused_computation.11 | convolution fusion | flops 51552190464 | bytes 50331648 | tf_op jit(solution)/shard_map/kxy,skyz->sxz/dot_general | solution.py:31
  306.4 113.6 %reduce-scatter.2.cloned.1.call-done = f32[2,128,1024]{1,2,0:T(8,128)} async-done(((f32[2,1024,1024]{1,2,0:T(8,128)}), f32[2,128,1024]{1,2,0:T(8,128)}) %reduce-scatter.2.cloned.1.call-update) | async-done | bytes 1048592 | tf_op jit(solution)/shard_map/reduce_scatter | solution.py:32
  420.1 2.0 copy.124
  422.1 18.2 %all_to_all.82 = f32[2,128,1024]{1,0,2:T(2,128)S(1)} all-to-all(f32[2,128,1024]{1,0,2:T(2,128)S(1)} %copy.124), channel_id=1, replica_groups=mesh['ia'=16,'ka'=8] {'ka'}, dimensions={2} | all-to-all | bytes 2097152 | tf_op jit(solution)/shard_map/all_to_all | solution.py:33
  440.3 0.3 copy.126
  440.7 1.3 copy.127
  442.0 7.6 %all-to-all-start.3 = ((f32[2,128,1024]{2,0,1:T(2,128)}), f32[2,128,1024]{2,0,1:T(2,128)S(1)}, u32[]{:S(2)}, u32[]{:S(2)}) async-start(f32[2,128,1024]{2,0,1:T(2,128)} %copy.127), calls=%async_computation.4 | async-start | bytes 2097152 | tf_op jit(solution)/shard_map/all_to_all | solution.py:35
  449.8 0.8 gather_fusion
  451.0 14.2 %all-to-all-done.3 = f32[2,128,1024]{2,0,1:T(2,128)S(1)} async-done(((f32[2,128,1024]{2,0,1:T(2,128)}), f32[2,128,1024]{2,0,1:T(2,128)S(1)}, u32[]{:S(2)}, u32[]{:S(2)}) %all-to-all-start.3) | async-done | bytes 1048608 | tf_op jit(solution)/shard_map/all_to_all | solution.py:35
  465.2 0.3 copy.150
  465.7 0.6 gather_fusion.1
  466.4 18.8 %all_to_all.83 = f32[16,2,8,1024]{3,2,1,0:T(8,128)S(1)} all-to-all(f32[16,2,8,1024]{3,2,1,0:T(8,128)S(1)} %broadcast_select_fusion), channel_id=1, replica_groups=mesh['ia'=16,'ka'=8] {'ia'}, dimensions={0} | all-to-all | bytes 2097152 | tf_op jit(solution)/shard_map/all_to_all | solution.py:42
  485.3 0.3 copy.132
  485.7 1.3 copy.133
  (25 shorter events, 1.2 us)
Async XLA Ops:
  136.6 107.1 %all-to-all-start.1 = ((f32[128,2,8,1024]{3,2,1,0:T(8,128)}), f32[128,2,8,1024]{3,2,1,0:T(8,128)}, u32[]{:S(2)}, u32[]{:S(2)}) async-start(f32[128,2,8,1024]{3,2,1,0:T(8,128)} %bitcast.94), calls=%async_computation.1 | async-start | bytes 16777216 | tf_op jit(solution)/shard_map/all_to_all | solution.py:22
  142.3 8.8 %copy-start.2 = (s32[1,2,2,8,8]{4,3,2,1,0:T(8,128)S(1)}, s32[1,2,2,8,8]{4,3,2,1,0:T(8,128)}, u32[]{:S(2)}) copy-start(s32[1,2,2,8,8]{4,3,2,1,0:T(8,128)} %param.6) | copy-start | bytes 3076
  142.3 277.8 %reduce-scatter.2.cloned.1.call-start = ((), (), s32[]{:S(2)}) async-start(), calls=%async_computation.6 | async-start | bytes 9437184 | tf_op jit(solution)/shard_map/reduce_scatter | solution.py:32
  306.4 143.2 %copy-start = (s32[16,2]{0,1:T(2,128)S(1)}, s32[16,2]{0,1:T(2,128)}, u32[]{:S(2)}) copy-start(s32[16,2]{0,1:T(2,128)} %param.7) | copy-start | bytes 388
  442.0 23.3 %all-to-all-start.3 = ((f32[2,128,1024]{2,0,1:T(2,128)}), f32[2,128,1024]{2,0,1:T(2,128)S(1)}, u32[]{:S(2)}, u32[]{:S(2)}) async-start(f32[2,128,1024]{2,0,1:T(2,128)} %copy.127), calls=%async_computation.4 | async-start | bytes 2097152 | tf_op jit(solution)/shard_map/all_to_all | solution.py:35
  450.5 35.1 %copy-start.1 = (f32[2,128,1024]{1,2,0:T(8,128)S(1)}, f32[2,128,1024]{1,2,0:T(8,128)}, u32[]{:S(2)}) copy-start(f32[2,128,1024]{1,2,0:T(8,128)} %reduce-scatter.2.cloned.1.call-done) | copy-start | bytes 3145732
Sparse Core Ops, SparseCore 0:
  306.5 113.4 reduce-scatter.1
where the time goes:
time: 495 us; the launch traced here: 494 us
  waiting for transfers between devices  196 us (40%)
  blocking collectives  146 us (29%)
  local copies, waits for them, and re-layouts  62.7 us (13%)
  matrix products  62.6 us (13%)
  between operations  13.5 us (3%)
  starting transfers between devices  13.3 us (3%)
    reduce_scatter x1, waiting for transfers between devices, body(): lax.psum_scatter(partial_value, 'ka', scatter_dimension=1, tiled=True)  114 us
    all_to_all x1, blocking collectives, mirror_direct(): lax.all_to_all(amplitudes, ('ia', 'ka'), split_axis=2, concat_axis=0, til...  109 us
    all_to_all x1, waiting for transfers between devices, mirror_direct(): lax.all_to_all(routed, ('ia', 'ka'), split_axis=0, concat_axis=2, tiled=T...  67.6 us
    dot_general x1, matrix products, body(): jnp.einsum('kxy,skyz->sxz', mixed, masked, precision=lax.Precision.HIGHEST)  62.6 us
    unnamed x8, local copies, waits for them, and re-layouts  23.1 us
    all_to_all x1, blocking collectives, body(): lax.all_to_all(routed, 'ia', split_axis=0, concat_axis=2, tiled=True)  18.8 us
    all_to_all x1, blocking collectives, body(): lax.all_to_all(own_rows, 'ka', split_axis=2, concat_axis=1, tiled=True)  18.2 us
    convert_element_type x1, local copies, waits for them, and re-layouts, expand_mask(): return grown.astype(jnp.float32)  18 us
  transfers between devices with their start and end apart: 3, of which 3 were waited for; matrix products, arithmetic and copies ran while one was open for 7% of the time, Pallas kernels for 0%

commit v1 on v0

v1 whole, which is shorter than its diff:
```python
import jax
import jax.numpy as jnp
from jax import lax
from jax.experimental import pallas as pl
from jax.experimental.pallas import tpu as pltpu
from jax.sharding import PartitionSpec as P

MESH = pl.DeviceIdType.MESH
HBM = pl.BlockSpec(memory_space=pl.ANY)

SIDE = 4
STEPS = ((1, 0, 0), (-1, 0, 0), (0, 1, 0), (0, -1, 0), (0, 0, 1), (0, 0, -1))
HOPS = 16
LAG = 2
SUBS = 2 * HOPS
CROSS_OWN = 3


def position():
    ia, ka = lax.axis_index("ia"), lax.axis_index("ka")
    return (ka % 2) * 2 + (ia // 2) % 2, ka // 2, ia // 4, ia % 2


def device(x, y, z, core):
    return z * 4 + (x % 2) * 2 + core, y * 2 + x // 2


def pick(test, then, other):
    return jnp.where(test, then, other)


def own_slot(index):
    return pick(index < CROSS_OWN, index, 2 * index - 2)


def relay_slot(index):
    return pick(index > 5, index + 8, 2 * index + 3)


def landing(x, y, z, half, index):
    apart = (z - y + SIDE) % SIDE
    inner = (x == 1) | (x == 2)
    x_way = pick(half == 0, 2 - x, x - 1)
    even = index % 2 == 0
    two_way = pick(half == 0, pick(even, 4, 5), pick(even, 2, 3))
    way = pick(
        apart == 0,
        pick(inner, x_way, 6 + half),
        pick(apart == 1, pick(half == 0, 4, 3), pick(apart == 3, pick(half == 0, 5, 2), two_way)),
    )
    slot = pick(apart == 2, relay_slot(index // 2), index)
    return way, slot


def mirror_kernel(t_ref, land, arrive, leave, swap_arrive, swap_leave):
    x, y, z, core = position()
    inner = (x == 1) | (x == 2)
    apart = (z - y + SIDE) % SIDE
    alone = (apart == 0) & jnp.logical_not(inner)

    def towards(way):
        dx, dy, dz = STEPS[way]
        return (x + dx + SIDE) % SIDE, (y + dy + SIDE) % SIDE, (z + dz + SIDE) % SIDE

    barrier = pltpu.get_barrier_semaphore()
    for way in range(6):
        for other in range(2):
            pl.semaphore_signal(barrier, inc=1, device_id=device(*towards(way), other), device_id_type=MESH)
    pl.semaphore_signal(barrier, inc=1, device_id=device(x, y, z, 1 - core), device_id_type=MESH)
    pl.semaphore_wait(barrier, 13)

    def swap(half):
        return pltpu.make_async_remote_copy(
            src_ref=t_ref.at[1 - core, pl.ds(half * HOPS, HOPS)],
            dst_ref=land.at[6 + half, :, core],
            send_sem=swap_leave.at[half],
            recv_sem=swap_arrive.at[half],
            device_id=device(x, y, z, 1 - core),
            device_id_type=MESH,
        )

    @pl.when(alone)
    def _():
        swap(0).start()
        swap(1).start()

    def landed(way, slot):
        pltpu.make_async_copy(land.at[way, slot], land.at[way, slot], arrive.at[way, slot]).wait()

    def send_own(way, slot, sub):
        for block in range(2):
            pltpu.make_async_remote_copy(
                src_ref=t_ref.at[block, sub],
                dst_ref=land.at[way, slot, core],
                send_sem=leave.at[way, slot],
                recv_sem=arrive.at[way, slot],
                device_id=device(*towards(way), block),
                device_id_type=MESH,
            ).start()

    def send_on(way, slot, from_way, from_slot):
        pltpu.make_async_remote_copy(
            src_ref=land.at[from_way, from_slot],
            dst_ref=land.at[way, slot],
            send_sem=leave.at[way, slot],
            recv_sem=arrive.at[way, slot],
            device_id=device(*towards(way), core),
            device_id_type=MESH,
        ).start()

    near_y = pick(inner, LAG, 0)
    near_z = pick(inner, 3 * LAG, 0)
    far_y = pick(inner, 4, 0)
    far_z = pick(inner, 4 + 2 * LAG, 0)

    relay_from = {2: (5, -1, 4, 4), 3: (4, 5, 5, -1), 4: (3, 2, 2, -1), 5: (2, -1, 3, 3)}

    def by_apart(values):
        zero, one, two, three = values
        return pick(apart == 0, zero, pick(apart == 1, one, pick(apart == 2, two, three)))

    def yz_lag(way):
        along_y = way < 4
        own, cross = (near_y, far_y) if along_y else (near_z, far_z)
        through = near_z if along_y else near_y
        passing = far_z if along_y else far_y
        values = [through + LAG, passing + LAG, cross, passing + LAG]
        for place, source in enumerate(relay_from[way]):
            if source < 0:
                values[place] = own
        return by_apart(values)

    lags = [
        pick(inner, 0, pick(x == 3, LAG, 2 * LAG)),
        pick(inner, 0, pick(x == 0, LAG, 2 * LAG)),
    ] + [yz_lag(way) for way in range(2, 6)]

    def step(t, carry):
        for way in range(6):
            slot = t - lags[way]
            active = (slot >= 0) & (slot < HOPS)
            if way < 2:
                half = pick(x == 1 + way, 0, 1)
                from_t, sub = inner, half * HOPS + slot
                from_way, from_slot = way, slot
            else:
                half = 0 if way < 4 else 1
                odd = way % 2
                early, late = slot < CROSS_OWN, slot > 13
                relayed = late | (jnp.logical_not(early) & (slot % 2 == 1))
                own_index = pick(early, slot, (slot + 2) // 2)
                relay_index = pick(late, slot - 8, (slot - 3) // 2)
                index = pick(apart == 2, 2 * own_index + odd, slot)
                places = relay_from[way]
                near_own = by_apart([places[0] < 0, places[1] < 0, False, places[3] < 0])
                own = pick(apart == 2, jnp.logical_not(relayed), near_own)
                from_t = own & jnp.logical_not(inner)
                sub = half * HOPS + index
                x_way = (2 - x) if half == 0 else (x - 1)
                relay_way = by_apart([max(place, 0) for place in places])
                from_way = pick(own, x_way, relay_way)
                from_slot = pick(own, index, pick(apart == 2, own_slot(relay_index), slot))

            @pl.when(active & from_t)
            def _(way=way, slot=slot, sub=sub):
                send_own(way, slot, sub)

            @pl.when(active & jnp.logical_not(from_t))
            def _(way=way, slot=slot, from_way=from_way, from_slot=from_slot):
                landed(from_way, from_slot)
                send_on(way, slot, from_way, from_slot)

        return carry

    lax.fori_loop(0, HOPS + 4 + 3 * LAG, step, 0)

    @pl.when(jnp.logical_not(alone))
    def _():
        def finish(index, carry):
            for half in range(2):
                landed(*landing(x, y, z, half, index))
            return carry

        lax.fori_loop(0, HOPS, finish, 0)

    @pl.when(alone)
    def _():
        swap(0).wait()
        swap(1).wait()

    def drain(slot, carry):
        for way in range(6):
            pltpu.make_async_copy(land.at[way, slot], land.at[way, slot], leave.at[way, slot]).wait()
        return carry

    lax.fori_loop(0, HOPS, drain, 0)


def mirror(amplitudes):
    blocks, virtuals = amplitudes.shape[0], amplitudes.shape[2]
    rows = virtuals // SUBS
    return pl.pallas_call(
        mirror_kernel,
        out_shape=jax.ShapeDtypeStruct((8, HOPS, blocks, rows, virtuals), jnp.float32),
        in_specs=[HBM],
        out_specs=HBM,
        scratch_shapes=[
            pltpu.SemaphoreType.DMA((6, HOPS)),
            pltpu.SemaphoreType.DMA((6, HOPS)),
            pltpu.SemaphoreType.DMA((2,)),
            pltpu.SemaphoreType.DMA((2,)),
        ],
        compiler_params=pltpu.CompilerParams(collective_id=0, has_side_effects=True),
    )(amplitudes.reshape(blocks, SUBS, rows, virtuals))


ROW_BLOCK = 256


def product_kernel(t_ref, land, w_ref, mask_ref, out_ref, t_buf, m_buf, w_buf, o_buf, t_sem, m_sem, w_sem, o_sem):
    x, y, z, core = position()
    alone = (z == y) & jnp.logical_not((x == 1) | (x == 2))
    blocks, virtuals = t_ref.shape[0], t_ref.shape[2]
    rows = virtuals // SUBS
    slots = w_ref.shape[0]
    tiles = 8
    tile = virtuals // tiles

    for block in range(blocks):
        pltpu.make_async_copy(t_ref.at[block], t_buf.at[block], t_sem.at[block]).start()

        @pl.when(alone & (core == block))
        def _(block=block):
            pltpu.make_async_copy(t_ref.at[block], m_buf.at[block], m_sem.at[block]).start()

        @pl.when(jnp.logical_not(alone & (core == block)))
        def _(block=block):
            def fetch(index, carry):
                for half in range(2):
                    way, slot = landing(x, y, z, half, index)
                    first = (half * HOPS + index) * rows
                    pltpu.make_async_copy(
                        land.at[way, slot, block],
                        m_buf.at[block, pl.ds(pl.multiple_of(first, rows), rows)],
                        m_sem.at[block],
                    ).start()
                return carry

            lax.fori_loop(0, HOPS, fetch, 0)

        for s in range(slots):
            pltpu.make_async_copy(w_ref.at[s, block], w_buf.at[s, block], w_sem.at[s, block]).start()

    for block in range(blocks):
        for s in range(slots):
            pltpu.make_async_copy(w_ref.at[s, block], w_buf.at[s, block], w_sem.at[s, block]).wait()

            def scale(r, carry, s=s, block=block):
                band = pl.ds(pl.multiple_of(r * tile, tile), tile)
                for c in range(tiles):
                    keep = mask_ref[((s * blocks + block) * tiles + r) * tiles + c]
                    columns = pl.ds(c * tile, tile)
                    value = w_buf[s, block, band, columns]
                    w_buf[s, block, band, columns] = jnp.where(keep != 0, value, jnp.zeros_like(value))
                return carry

            lax.fori_loop(0, tiles, scale, 0)

    for block in range(blocks):
        pltpu.make_async_copy(t_ref.at[block], t_buf.at[block], t_sem.at[block]).wait()
        pltpu.make_async_copy(t_ref.at[block], m_buf.at[block], m_sem.at[block]).wait()

    def band_of(b, carry):
        band = pl.ds(pl.multiple_of(b * ROW_BLOCK, ROW_BLOCK), ROW_BLOCK)
        halves = []
        for block in range(blocks):
            mixed = 2.0 * t_buf[block, band, :] - m_buf[block, :, band].T
            high = mixed.astype(jnp.bfloat16)
            low = (mixed - high.astype(jnp.float32)).astype(jnp.bfloat16)
            halves.append(jnp.concatenate([high, low], axis=0))
        for s in range(slots):
            total = jnp.zeros((2 * ROW_BLOCK, virtuals), jnp.float32)
            for block in range(blocks):
                total += jnp.dot(halves[block], w_buf[s, block], preferred_element_type=jnp.float32)
            o_buf[s, band, :] = total[:ROW_BLOCK] + total[ROW_BLOCK:]
            pltpu.make_async_copy(o_buf.at[s, band], out_ref.at[s, band], o_sem.at[s, b]).start()
        return carry

    bands = virtuals // ROW_BLOCK
    lax.fori_loop(0, bands, band_of, 0)
    for b in range(bands):
        for s in range(slots):
            band = pl.ds(b * ROW_BLOCK, ROW_BLOCK)
            pltpu.make_async_copy(o_buf.at[s, band], out_ref.at[s, band], o_sem.at[s, b]).wait()


def product(amplitudes, land, integrals, tile_mask):
    slots, blocks, virtuals = integrals.shape[0], integrals.shape[1], integrals.shape[2]
    return pl.pallas_call(
        product_kernel,
        out_shape=jax.ShapeDtypeStruct((slots, virtuals, virtuals), jnp.float32),
        in_specs=[HBM, HBM, HBM, pl.BlockSpec(memory_space=pltpu.SMEM)],
        out_specs=HBM,
        scratch_shapes=[
            pltpu.VMEM((blocks, virtuals, virtuals), jnp.float32),
            pltpu.VMEM((blocks, virtuals, virtuals), jnp.float32),
            pltpu.VMEM((slots, blocks, virtuals, virtuals), jnp.bfloat16),
            pltpu.VMEM((slots, virtuals, virtuals), jnp.float32),
            pltpu.SemaphoreType.DMA((blocks,)),
            pltpu.SemaphoreType.DMA((blocks,)),
            pltpu.SemaphoreType.DMA((slots, blocks)),
            pltpu.SemaphoreType.DMA((slots, virtuals // ROW_BLOCK)),
        ],
        compiler_params=pltpu.CompilerParams(vmem_limit_bytes=58 << 20),
    )(amplitudes, land, integrals, tile_mask.reshape(-1))


def body(amplitudes, integrals, tile_mask, pair_list):
    land = mirror(amplitudes[0])
    partial_value = product(amplitudes[0], land, integrals[0], tile_mask[0])
    own_rows = lax.psum_scatter(partial_value, "ka", scatter_dimension=1, tiled=True)
    columns = lax.all_to_all(own_rows, "ka", split_axis=2, concat_axis=1, tiled=True)
    flipped = jnp.swapaxes(columns, 1, 2)
    spread = lax.all_to_all(flipped, "ia", split_axis=1, concat_axis=0, tiled=True)
    occupied = pair_list.shape[0]
    owners = jnp.arange(occupied, dtype=jnp.int32)
    partner_slot = jnp.where(pair_list[pair_list, 0] == owners[:, None], 0, 1).astype(jnp.int32)
    source_row = pair_list * 2 + partner_slot
    routed = jnp.take(spread, source_row.reshape(-1), axis=0)
    routed = routed.reshape(occupied, 2, spread.shape[1], spread.shape[2])
    delivered = lax.all_to_all(routed, "ia", split_axis=0, concat_axis=2, tiled=True)
    return (own_rows + delivered[0])[None]


def solution(mesh):
    placed = (
        P("ia", "ka", None, None),
        P("ia", None, "ka", None, None),
        P("ia", None, "ka", None, None),
        P(),
    )
    return jax.shard_map(
        body, mesh=mesh, in_specs=placed, out_specs=P("ia", None, "ka", None), check_vma=False
    )
```

time: 495 us -> 373 us (0.75)
  Pallas kernels: 0 us -> 141 us
  blocking collectives: 146 us -> 36.9 us
  matrix products: 62.6 us -> 0 us
  local copies, waits for them, and re-layouts: 62.7 us -> 6.29 us
  waiting for transfers between devices: 196 us -> 166 us
  starting transfers between devices: 13.3 us -> 7.63 us
    pallas_call x0 -> x2, Pallas kernels: none -> 141 us  [the longest x1 112 us: mirror(): pl.pallas_call(mirror_kernel, out_shape=jax.ShapeDtypeStruct((8, HOPS, bl...]
    all_to_all x1 -> x0, blocking collectives: 109 us -> none  [mirror_direct(): lax.all_to_all(amplitudes, ('ia', 'ka'), split_axis=2, concat_axis=0, til...]
    all_to_all x1 -> x0, waiting for transfers between devices: 67.6 us -> none  [mirror_direct(): lax.all_to_all(routed, ('ia', 'ka'), split_axis=0, concat_axis=2, tiled=T...]
    dot_general x1 -> x0, matrix products: 62.6 us -> none  [body(): jnp.einsum('kxy,skyz->sxz', mixed, masked, precision=lax.Precision.HIGHEST)]
    reduce_scatter x1, waiting for transfers between devices: 114 us -> 152 us  [body(): lax.psum_scatter(partial_value, 'ka', scatter_dimension=1, tiled=True)]
    unnamed x8 -> x6, local copies, waits for them, and re-layouts: 23.1 us -> 0.01 us
    convert_element_type x1 -> x0, local copies, waits for them, and re-layouts: 18 us -> none  [expand_mask(): return grown.astype(jnp.float32)]
    broadcast_in_dim x3 -> x0, local copies, waits for them, and re-layouts: 8.37 us -> none  [the longest x1 6.92 us: expand_mask(): jnp.repeat(jnp.repeat(tile_mask, tile_side, axis=-2), tile_side, axis=-1)]
  transfers between devices with their start and end apart: 3 -> 2, of which waited for: 3 -> 2; matrix products, arithmetic and copies ran while one was open for 7% -> 0% of each run, Pallas kernels for 0% -> 0%
where the time goes in v1:
time: 373 us
  waiting for transfers between devices  166 us (45%)
  Pallas kernels  141 us (38%)
  blocking collectives  36.9 us (10%)
  between operations  13.5 us (4%)
  starting transfers between devices  7.63 us (2%)
  local copies, waits for them, and re-layouts  6.29 us (2%)
    reduce_scatter x1, waiting for transfers between devices, body(): lax.psum_scatter(partial_value, 'ka', scatter_dimension=1, tiled=True)  152 us
    pallas_call x1, Pallas kernels, mirror(): pl.pallas_call(mirror_kernel, out_shape=jax.ShapeDtypeStruct((8, HOPS, bl...  112 us
    pallas_call x1, Pallas kernels, product(): pl.pallas_call(product_kernel, out_shape=jax.ShapeDtypeStruct((slots, vir...  29 us
    all_to_all x1, blocking collectives, body(): lax.all_to_all(routed, 'ia', split_axis=0, concat_axis=2, tiled=True)  18.8 us
    all_to_all x1, blocking collectives, body(): lax.all_to_all(own_rows, 'ka', split_axis=2, concat_axis=1, tiled=True)  18.1 us
    all_to_all x1, waiting for transfers between devices, body(): lax.all_to_all(flipped, 'ia', split_axis=1, concat_axis=0, tiled=True)  14.2 us
    all_to_all x1, starting transfers between devices, body(): lax.all_to_all(flipped, 'ia', split_axis=1, concat_axis=0, tiled=True)  7.63 us
  transfers between devices with their start and end apart: 2, of which 2 were waited for; matrix products, arithmetic and copies ran while one was open for 0% of the time, Pallas kernels for 0%

profile of v1, /device:TPU:1, one launch (start us, length us, event | category | flops | bytes accessed | tf_op | source)
XLA Modules:
  0.0 372.8 jit_solution(15928897836035551928)
XLA Ops:
  6.5 112.3 %shard_map.46.land = f32[8,16,2,32,1024]{4,3,2,1,0:T(8,128)} custom-call(f32[2,32,32,1024]{3,2,1,0:T(8,128)} %bitcast.31), custom_call_target="tpu_custom_call" | custom-call | tf_op jit(solution)/shard_map/pallas_call | solution.py:202
  118.9 0.7 reshape_squeeze.7.mask_ref
  119.5 29.0 %shard_map.47 = f32[2,1024,1024]{2,1,0:T(8,128)} custom-call(f32[2,1024,1024]{2,1,0:T(8,128)} %bitcast.32, f32[8,16,2,32,1024]{4,3,2,1,0:T(8,128)} %shard_map.46.land, bf16[2,2,1024,1024]{3,2,1,0:T(8,128)(2,1)} %bitcast.33, s32[256]{0:T(256)} %reshape_squeeze.7.mask_ref), custom_call_target="tpu_custom_call" | custom-call | tf_op jit(solution)/shard_map/pallas_call | solution.py:299
  148.5 151.7 %reduce-scatter.2.cloned.1.call-done = f32[2,128,1024]{2,1,0:T(8,128)} async-done(((f32[2,1024,1024]{2,1,0:T(8,128)}), f32[2,128,1024]{2,1,0:T(8,128)}) %reduce-scatter.2.cloned.1.call-update) | async-done | bytes 1048592 | tf_op jit(solution)/shard_map/reduce_scatter | solution.py:321
  300.2 1.5 copy.53
  301.7 18.1 %all_to_all.51 = f32[2,128,1024]{1,0,2:T(2,128)S(1)} all-to-all(f32[2,128,1024]{1,0,2:T(2,128)S(1)} %copy.53), channel_id=1, replica_groups=mesh['ia'=16,'ka'=8] {'ka'}, dimensions={2} | all-to-all | bytes 2097152 | tf_op jit(solution)/shard_map/all_to_all | solution.py:322
  320.0 0.3 copy.55
  320.3 1.3 copy.56
  321.6 7.6 %all-to-all-start.1 = ((f32[2,128,1024]{2,0,1:T(2,128)}), f32[2,128,1024]{2,0,1:T(2,128)S(1)}, u32[]{:S(2)}, u32[]{:S(2)}) async-start(f32[2,128,1024]{2,0,1:T(2,128)} %copy.56), calls=%async_computation.2 | async-start | bytes 2097152 | tf_op jit(solution)/shard_map/all_to_all | solution.py:324
  329.2 0.1 copy.50
  329.3 0.1 reshape.42
  329.4 0.8 gather_fusion
  330.2 0.1 reshape.45
  330.3 0.1 copy.51
  330.4 0.1 copy.59
  330.5 0.1 reshape.41
  330.5 0.1 copy.52
  330.7 14.2 %all-to-all-done.1 = f32[2,128,1024]{2,0,1:T(2,128)S(1)} async-done(((f32[2,128,1024]{2,0,1:T(2,128)}), f32[2,128,1024]{2,0,1:T(2,128)S(1)}, u32[]{:S(2)}, u32[]{:S(2)}) %all-to-all-start.1) | async-done | bytes 1048608 | tf_op jit(solution)/shard_map/all_to_all | solution.py:324
  344.9 0.3 copy.63
  345.2 0.1 copy.58
  345.3 0.6 gather_fusion.1
  345.9 0.1 broadcast_select_fusion
  346.1 18.8 %all_to_all.52 = f32[16,2,8,1024]{3,2,1,0:T(8,128)S(1)} all-to-all(f32[16,2,8,1024]{3,2,1,0:T(8,128)S(1)} %broadcast_select_fusion), channel_id=1, replica_groups=mesh['ia'=16,'ka'=8] {'ia'}, dimensions={0} | all-to-all | bytes 2097152 | tf_op jit(solution)/shard_map/all_to_all | solution.py:331
  364.9 1.1 fusion
  (13 shorter events, 0.1 us)
Async XLA Ops:
  6.5 293.7 %reduce-scatter.2.cloned.1.call-start = ((), (), s32[]{:S(2)}) async-start(), calls=%async_computation.4 | async-start | bytes 9437184 | tf_op jit(solution)/shard_map/reduce_scatter | solution.py:321
  6.5 112.3 %copy-start.2 = (s32[1,2,2,8,8]{4,3,2,1,0:T(8,128)S(1)}, s32[1,2,2,8,8]{4,3,2,1,0:T(8,128)}, u32[]{:S(2)}) copy-start(s32[1,2,2,8,8]{4,3,2,1,0:T(8,128)} %param.6) | copy-start | bytes 3076
  148.5 180.7 %copy-start = (s32[16,2]{0,1:T(2,128)S(1)}, s32[16,2]{0,1:T(2,128)}, u32[]{:S(2)}) copy-start(s32[16,2]{0,1:T(2,128)} %param.7) | copy-start | bytes 388
  321.6 23.3 %all-to-all-start.1 = ((f32[2,128,1024]{2,0,1:T(2,128)}), f32[2,128,1024]{2,0,1:T(2,128)S(1)}, u32[]{:S(2)}, u32[]{:S(2)}) async-start(f32[2,128,1024]{2,0,1:T(2,128)} %copy.56), calls=%async_computation.2 | async-start | bytes 2097152 | tf_op jit(solution)/shard_map/all_to_all | solution.py:324
  329.4 35.4 %copy-start.1 = (f32[2,128,1024]{2,1,0:T(8,128)S(1)}, f32[2,128,1024]{2,1,0:T(8,128)}, u32[]{:S(2)}) copy-start(f32[2,128,1024]{2,1,0:T(8,128)} %reduce-scatter.2.cloned.1.call-done) | copy-start | bytes 3145732
Sparse Core Ops, SparseCore 0:
  148.7 151.5 reduce-scatter.1

commit v2 on v1

v2 whole, which is shorter than its diff:
```python
import jax
import jax.numpy as jnp
from jax import lax
from jax.experimental import pallas as pl
from jax.experimental.pallas import tpu as pltpu
from jax.sharding import PartitionSpec as P

MESH = pl.DeviceIdType.MESH
HBM = pl.BlockSpec(memory_space=pl.ANY)

SIDE = 4
STEPS = ((1, 0, 0), (-1, 0, 0), (0, 1, 0), (0, -1, 0), (0, 0, 1), (0, 0, -1))
HOPS = 32
LAG = 2
SUBS = 2 * HOPS
CROSS_OWN = 3
BAND = 256
CHUNKS = 4


def position():
    ia, ka = lax.axis_index("ia"), lax.axis_index("ka")
    return (ka % 2) * 2 + (ia // 2) % 2, ka // 2, ia // 4, ia % 2


def towards(x, y, z, way):
    dx, dy, dz = STEPS[way]
    return (x + dx + SIDE) % SIDE, (y + dy + SIDE) % SIDE, (z + dz + SIDE) % SIDE


def device(x, y, z, core):
    return z * 4 + (x % 2) * 2 + core, y * 2 + x // 2


def pick(test, then, other):
    return jnp.where(test, then, other)


def own_slot(index):
    return pick(index < CROSS_OWN, index, 2 * index - 2)


def relay_slot(index):
    return pick(index > HOPS // 2 - 3, index + HOPS // 2, 2 * index + 3)


def landing(x, y, z, half, index):
    apart = (z - y + SIDE) % SIDE
    x_way = pick(half == 0, 2 - x, x - 1)
    even = index % 2 == 0
    two_way = pick(half == 0, pick(even, 4, 5), pick(even, 2, 3))
    way = pick(
        apart == 0,
        x_way,
        pick(apart == 1, pick(half == 0, 4, 3), pick(apart == 3, pick(half == 0, 5, 2), two_way)),
    )
    slot = pick(apart == 2, relay_slot(index // 2), index)
    return way, slot


def exchange(t_ref, land, m_buf, arrive, leave, m_sem, swap_arrive, swap_leave):
    x, y, z, core = position()
    inner = (x == 1) | (x == 2)
    apart = (z - y + SIDE) % SIDE
    alone = (apart == 0) & jnp.logical_not(inner)

    def swap(half):
        return pltpu.make_async_remote_copy(
            src_ref=t_ref.at[1 - core, pl.ds(half * HOPS, HOPS)],
            dst_ref=m_buf.at[core, pl.ds(half * HOPS, HOPS)],
            send_sem=swap_leave.at[half],
            recv_sem=swap_arrive.at[half],
            device_id=device(x, y, z, 1 - core),
            device_id_type=MESH,
        )

    @pl.when(alone)
    def _():
        swap(0).start()
        swap(1).start()
        pltpu.make_async_copy(t_ref.at[core], m_buf.at[core], m_sem).start()

    def landed(way, slot):
        pltpu.make_async_copy(land.at[way, slot], land.at[way, slot], arrive.at[way, slot]).wait()

    def send_own(way, slot, sub):
        for block in range(2):
            pltpu.make_async_remote_copy(
                src_ref=t_ref.at[block, sub],
                dst_ref=land.at[way, slot, core],
                send_sem=leave.at[way, slot],
                recv_sem=arrive.at[way, slot],
                device_id=device(*towards(x, y, z, way), block),
                device_id_type=MESH,
            ).start()

    def send_on(way, slot, from_way, from_slot):
        pltpu.make_async_remote_copy(
            src_ref=land.at[from_way, from_slot],
            dst_ref=land.at[way, slot],
            send_sem=leave.at[way, slot],
            recv_sem=arrive.at[way, slot],
            device_id=device(*towards(x, y, z, way), core),
            device_id_type=MESH,
        ).start()

    near_y = pick(inner, LAG, 0)
    near_z = pick(inner, 3 * LAG, 0)
    far_y = pick(inner, 4, 0)
    far_z = pick(inner, 4 + 2 * LAG, 0)

    relay_from = {2: (5, -1, 4, 4), 3: (4, 5, 5, -1), 4: (3, 2, 2, -1), 5: (2, -1, 3, 3)}

    def by_apart(values):
        zero, one, two, three = values
        return pick(apart == 0, zero, pick(apart == 1, one, pick(apart == 2, two, three)))

    def yz_lag(way):
        along_y = way < 4
        own, cross = (near_y, far_y) if along_y else (near_z, far_z)
        through = near_z if along_y else near_y
        passing = far_z if along_y else far_y
        values = [through + LAG, passing + LAG, cross, passing + LAG]
        for place, source in enumerate(relay_from[way]):
            if source < 0:
                values[place] = own
        return by_apart(values)

    lags = [
        pick(inner, 0, pick(x == 3, LAG, 2 * LAG)),
        pick(inner, 0, pick(x == 0, LAG, 2 * LAG)),
    ] + [yz_lag(way) for way in range(2, 6)]

    def step(t, carry):
        for way in range(6):
            slot = t - lags[way]
            active = (slot >= 0) & (slot < HOPS)
            if way < 2:
                half = pick(x == 1 + way, 0, 1)
                from_t, sub = inner, half * HOPS + slot
                from_way, from_slot = way, slot
            else:
                half = 0 if way < 4 else 1
                odd = way % 2
                early, late = slot < CROSS_OWN, slot > HOPS - 3
                relayed = late | (jnp.logical_not(early) & (slot % 2 == 1))
                own_index = pick(early, slot, (slot + 2) // 2)
                relay_index = pick(late, slot - HOPS // 2, (slot - 3) // 2)
                index = pick(apart == 2, 2 * own_index + odd, slot)
                places = relay_from[way]
                near_own = by_apart([places[0] < 0, places[1] < 0, False, places[3] < 0])
                own = pick(apart == 2, jnp.logical_not(relayed), near_own)
                from_t = own & jnp.logical_not(inner)
                sub = half * HOPS + index
                x_way = (2 - x) if half == 0 else (x - 1)
                relay_way = by_apart([max(place, 0) for place in places])
                from_way = pick(own, x_way, relay_way)
                from_slot = pick(own, index, pick(apart == 2, own_slot(relay_index), slot))

            @pl.when(active & from_t)
            def _(way=way, slot=slot, sub=sub):
                send_own(way, slot, sub)

            @pl.when(active & jnp.logical_not(from_t))
            def _(way=way, slot=slot, from_way=from_way, from_slot=from_slot):
                landed(from_way, from_slot)
                send_on(way, slot, from_way, from_slot)

        return carry

    lax.fori_loop(0, HOPS + 4 + 3 * LAG, step, 0)

    @pl.when(jnp.logical_not(alone))
    def _():
        def finish(index, carry):
            for half in range(2):
                way, slot = landing(x, y, z, half, index)
                landed(way, slot)
                pltpu.make_async_copy(land.at[way, slot], m_buf.at[:, half * HOPS + index], m_sem).start()
            return carry

        lax.fori_loop(0, HOPS, finish, 0)
        pltpu.make_async_copy(m_buf, m_buf, m_sem).wait()

    @pl.when(alone)
    def _():
        swap(0).wait()
        swap(1).wait()
        pltpu.make_async_copy(t_ref.at[core], m_buf.at[core], m_sem).wait()


def drain_exchange(land, leave):
    def drain(slot, carry):
        for way in range(6):
            pltpu.make_async_copy(land.at[way, slot], land.at[way, slot], leave.at[way, slot]).wait()
        return carry

    lax.fori_loop(0, HOPS, drain, 0)


def cycle_kernel(
    t_ref, w_ref, mask_ref, land, out_ref,
    t_buf, m_buf, w_buf, o_buf, ring, relay, inbox,
    arrive, leave, t_sem, m_sem, w_sem, swap_arrive, swap_leave,
    ring_arrive, ring_leave, relay_arrive, relay_leave, inbox_arrive, inbox_leave,
):
    x, y, z, core = position()
    slots, blocks, virtuals = w_buf.shape[0], w_buf.shape[1], w_buf.shape[2]

    barrier = pltpu.get_barrier_semaphore()
    for way in range(6):
        for other in range(2):
            pl.semaphore_signal(
                barrier, inc=1, device_id=device(*towards(x, y, z, way), other), device_id_type=MESH
            )
    pl.semaphore_signal(barrier, inc=1, device_id=device(x, y, z, 1 - core), device_id_type=MESH)
    pl.semaphore_wait(barrier, 13)

    load_t = pltpu.make_async_copy(t_ref, t_buf, t_sem)
    load_w = pltpu.make_async_copy(w_ref, w_buf, w_sem)
    load_t.start()
    load_w.start()

    exchange(t_ref, land, m_buf, arrive, leave, m_sem, swap_arrive, swap_leave)

    load_t.wait()
    load_w.wait()
    tiles = 8
    tile = virtuals // tiles

    def mask_band(n, carry):
        s, block, r = n // (blocks * tiles), (n // tiles) % blocks, n % tiles
        band = pl.ds(pl.multiple_of(r * tile, tile), tile)
        for c in range(tiles):
            keep = mask_ref[n * tiles + c]
            columns = pl.ds(c * tile, tile)
            value = w_buf[s, block, band, columns]
            w_buf[s, block, band, columns] = jnp.where(keep != 0, value, jnp.zeros_like(value))
        return carry

    lax.fori_loop(0, slots * blocks * tiles, mask_band, 0)

    x_half = x // 2
    part = BAND // CHUNKS

    def band_of(s, k):
        return pick(s == 0, y + SIDE - 1 - k, y + 1 + k) % SIDE

    def rows_of(band, chunk):
        offset = pick(chunk < 2, (1 - x_half) * (BAND // 2), x_half * (BAND // 2) - BAND // 2) + chunk * part
        return pl.ds(pl.multiple_of(band * BAND + offset, part), part)

    def ring_copy(s, k, chunk):
        return pltpu.make_async_remote_copy(
            src_ref=o_buf.at[s, rows_of(band_of(s, k), chunk)],
            dst_ref=ring.at[s, k, chunk],
            send_sem=ring_leave.at[s, k, chunk],
            recv_sem=ring_arrive.at[s, k, chunk],
            device_id=device(x, (y + pick(s == 0, 1, SIDE - 1)) % SIDE, z, core),
            device_id_type=MESH,
        )

    def x_beside(s):
        return device((x + pick(s == 0, 1, SIDE - 1)) % SIDE, y, z, core)

    def relay_copy(s, chunk):
        return pltpu.make_async_remote_copy(
            src_ref=o_buf.at[s, rows_of(y, chunk)],
            dst_ref=relay.at[s, chunk],
            send_sem=relay_leave.at[s, chunk],
            recv_sem=relay_arrive.at[s, chunk],
            device_id=x_beside(s),
            device_id_type=MESH,
        )

    def inbox_copy(s, chunk):
        return pltpu.make_async_remote_copy(
            src_ref=relay.at[s, chunk],
            dst_ref=inbox.at[s, chunk],
            send_sem=inbox_leave.at[s, chunk],
            recv_sem=inbox_arrive.at[s, chunk],
            device_id=x_beside(s),
            device_id_type=MESH,
        )

    def absorb(s, k, chunk):
        ring_copy(s, k - 1, chunk).wait_recv()
        rows = rows_of(band_of(s, k), chunk)
        o_buf[s, rows, :] = o_buf[s, rows, :] + ring[s, k - 1, chunk]

    def unit(u, carry):
        s = u % 2
        band = pl.ds(pl.multiple_of(band_of(s, u // 2) * BAND, BAND), BAND)
        total = jnp.zeros((2 * BAND, virtuals), jnp.float32)
        for block in range(blocks):
            mirrored = m_buf[block, :, :, band].reshape(virtuals, BAND).T
            mixed = 2.0 * t_rows(block, u) - mirrored
            high = mixed.astype(jnp.bfloat16)
            low = (mixed - high.astype(jnp.float32)).astype(jnp.bfloat16)
            pair = jnp.concatenate([high, low], axis=0)
            total += jnp.dot(pair, w_buf[s, block], preferred_element_type=jnp.float32)
        o_buf[s, band, :] = total[:BAND] + total[BAND:]

        @pl.when(u < 2)
        def _():
            for chunk in range(CHUNKS):
                ring_copy(s, 0, chunk).start()

        @pl.when((u >= 3) & (u < 3 + CHUNKS))
        def _():
            for way in range(2):
                absorb(way, 1, u - 3)
                ring_copy(way, 1, u - 3).start()

        return carry

    def t_rows(block, u):
        band = band_of(u % 2, u // 2)
        subs = BAND // t_buf.shape[2]
        return t_buf[block, pl.ds(band * subs, subs)].reshape(BAND, virtuals)

    lax.fori_loop(0, slots * SIDE, unit, 0)

    def second(chunk, carry):
        for s in range(2):
            absorb(s, 2, chunk)
            ring_copy(s, 2, chunk).start()
        return carry

    lax.fori_loop(0, CHUNKS, second, 0)

    def third(chunk, carry):
        for s in range(2):
            absorb(s, 3, chunk)

        @pl.when(chunk < 2)
        def _():
            for s in range(2):
                relay_copy(s, chunk).start()

        @pl.when(chunk >= 2)
        def _():
            for s in range(2):
                relay_copy(s, chunk - 2).wait_recv()
                inbox_copy(s, chunk - 2).start()

        return carry

    lax.fori_loop(0, CHUNKS, third, 0)

    for chunk in range(2):
        for s in range(2):
            inbox_copy(s, chunk).wait_recv()
            out_ref[s, pl.ds(chunk * part, part), :] = o_buf[s, rows_of(y, chunk + 2), :] + inbox[s, chunk]

    def drain(chunk, carry):
        for s in range(2):
            for k in range(3):
                ring_copy(s, k, chunk).wait_send()
        return carry

    lax.fori_loop(0, CHUNKS, drain, 0)
    for chunk in range(2):
        for s in range(2):
            relay_copy(s, chunk).wait_send()
            inbox_copy(s, chunk).wait_send()
    drain_exchange(land, leave)


def summed_rows(amplitudes, integrals, tile_mask):
    slots, blocks, virtuals = integrals.shape[0], integrals.shape[1], integrals.shape[2]
    rows = virtuals // SUBS
    part = BAND // CHUNKS
    dma = pltpu.SemaphoreType.DMA
    return pl.pallas_call(
        cycle_kernel,
        out_shape=(
            jax.ShapeDtypeStruct((6, HOPS, blocks, rows, virtuals), jnp.float32),
            jax.ShapeDtypeStruct((slots, BAND // 2, virtuals), jnp.float32),
        ),
        in_specs=[HBM, HBM, pl.BlockSpec(memory_space=pltpu.SMEM)],
        out_specs=(HBM, pl.BlockSpec(memory_space=pltpu.VMEM)),
        scratch_shapes=[
            pltpu.VMEM((blocks, SUBS, rows, virtuals), jnp.float32),
            pltpu.VMEM((blocks, SUBS, rows, virtuals), jnp.float32),
            pltpu.VMEM((slots, blocks, virtuals, virtuals), jnp.bfloat16),
            pltpu.VMEM((slots, virtuals, virtuals), jnp.float32),
            pltpu.VMEM((slots, 3, CHUNKS, part, virtuals), jnp.float32),
            pltpu.VMEM((slots, 2, part, virtuals), jnp.float32),
            pltpu.VMEM((slots, 2, part, virtuals), jnp.float32),
            dma((6, HOPS)),
            dma((6, HOPS)),
            dma,
            dma,
            dma,
            dma((2,)),
            dma((2,)),
            dma((slots, 3, CHUNKS)),
            dma((slots, 3, CHUNKS)),
            dma((slots, 2)),
            dma((slots, 2)),
            dma((slots, 2)),
            dma((slots, 2)),
        ],
        compiler_params=pltpu.CompilerParams(
            collective_id=0, has_side_effects=True, vmem_limit_bytes=58 << 20
        ),
    )(amplitudes.reshape(blocks, SUBS, rows, virtuals), integrals, tile_mask.reshape(-1))[1]


def body(amplitudes, integrals, tile_mask, pair_list):
    own_rows = summed_rows(amplitudes[0], integrals[0], tile_mask[0])
    row_groups, col_groups = lax.axis_size("ia"), lax.axis_size("ka")
    slots, rows, virtuals = own_rows.shape
    thin, wide = rows // row_groups, virtuals // col_groups
    pieces = own_rows.reshape(slots, row_groups, thin, col_groups, wide).transpose(1, 3, 0, 2, 4)
    pieces = pieces.reshape(row_groups * col_groups, slots, thin, wide)
    spread = lax.all_to_all(pieces, ("ia", "ka"), split_axis=0, concat_axis=0, tiled=True)
    spread = spread.reshape(row_groups, col_groups, slots, thin, wide).transpose(0, 2, 1, 3, 4)
    spread = spread.reshape(row_groups * slots, col_groups, thin, wide)
    owners = jnp.arange(row_groups, dtype=jnp.int32)
    partner_slot = jnp.where(pair_list[pair_list, 0] == owners[:, None], 0, 1).astype(jnp.int32)
    source_row = pair_list * 2 + partner_slot
    routed = jnp.take(spread, source_row.reshape(-1), axis=0)
    routed = routed.reshape(row_groups, slots, col_groups, thin, wide)
    delivered = lax.all_to_all(routed, "ia", split_axis=0, concat_axis=0, tiled=True)
    mirrored = delivered.transpose(1, 4, 2, 0, 3).reshape(slots, wide, virtuals)
    return (own_rows + mirrored)[None]


def solution(mesh):
    placed = (
        P("ia", "ka", None, None),
        P("ia", None, "ka", None, None),
        P("ia", None, "ka", None, None),
        P(),
    )
    return jax.shard_map(
        body, mesh=mesh, in_specs=placed, out_specs=P("ia", None, "ka", None), check_vma=False
    )
```

time: 373 us -> 273 us (0.73)
  waiting for transfers between devices: 166 us -> 18.1 us
  Pallas kernels: 141 us -> 219 us
  blocking collectives: 36.9 us -> 18 us
  between operations: 13.5 us -> 0.1 us
    reduce_scatter x1 -> x0, waiting for transfers between devices: 152 us -> none  [body(): lax.psum_scatter(partial_value, 'ka', scatter_dimension=1, tiled=True)]
    pallas_call x2 -> x1, Pallas kernels: 141 us -> 219 us  [summed_rows(): pl.pallas_call(cycle_kernel, out_shape=(jax.ShapeDtypeStruct((6, HOPS, bl...]
    all_to_all x2 -> x1, blocking collectives: 36.9 us -> 18 us  [body(): lax.all_to_all(routed, 'ia', split_axis=0, concat_axis=0, tiled=True)]
    all_to_all x1, waiting for transfers between devices: 14.2 us -> 18.1 us  [body(): lax.all_to_all(pieces, ('ia', 'ka'), split_axis=0, concat_axis=0, tiled=T...]
  transfers between devices with their start and end apart: 2 -> 1, of which waited for: 2 -> 1; matrix products, arithmetic and copies ran while one was open for 0% -> 1% of each run, Pallas kernels for 0% -> 0%
where the time goes in v2:
time: 273 us
  Pallas kernels  219 us (80%)
  waiting for transfers between devices  18.1 us (7%)
  blocking collectives  18 us (7%)
  starting transfers between devices  10.5 us (4%)
  local copies, waits for them, and re-layouts  6.2 us (2%)
    pallas_call x1, Pallas kernels, summed_rows(): pl.pallas_call(cycle_kernel, out_shape=(jax.ShapeDtypeStruct((6, HOPS, bl...  219 us
    all_to_all x1, waiting for transfers between devices, body(): lax.all_to_all(pieces, ('ia', 'ka'), split_axis=0, concat_axis=0, tiled=T...  18.1 us
    all_to_all x1, blocking collectives, body(): lax.all_to_all(routed, 'ia', split_axis=0, concat_axis=0, tiled=True)  18 us
    all_to_all x1, starting transfers between devices, body(): lax.all_to_all(pieces, ('ia', 'ka'), split_axis=0, concat_axis=0, tiled=T...  10.5 us
  transfers between devices with their start and end apart: 1, of which 1 were waited for; matrix products, arithmetic and copies ran while one was open for 1% of the time, Pallas kernels for 0%

profile of v2, /device:TPU:1, one launch (start us, length us, event | category | flops | bytes accessed | tf_op | source)
XLA Modules:
  0.0 272.9 jit_solution(14413033675637399866)
XLA Ops:
  0.0 1.4 reshape_squeeze.7.mask_ref
  1.4 0.0 copy-start
  1.4 218.7 %shard_map.46 = (f32[6,32,2,16,1024]{4,3,2,1,0:T(8,128)}, f32[2,128,1024]{2,1,0:T(8,128)}) custom-call(f32[2,64,16,1024]{3,2,1,0:T(8,128)} %bitcast.19, bf16[2,2,1024,1024]{3,2,1,0:T(8,128)(2,1)} %bitcast.20, s32[256]{0:T(256)} %reshape_squeeze.7.mask_ref), custom_call_target="tpu_custom_call" | custom-call | tf_op jit(solution)/shard_map/pallas_call | solution.py:375
  220.1 2.3 copy.36
  222.4 10.5 %all-to-all-start = ((f32[128,2,8,128]{3,2,1,0:T(8,128)}), f32[128,2,8,128]{3,2,1,0:T(8,128)S(1)}, u32[]{:S(2)}, u32[]{:S(2)}) async-start(f32[128,2,8,128]{3,2,1,0:T(8,128)} %bitcast.4), calls=%async_computation | async-start | bytes 2097152 | tf_op jit(solution)/shard_map/all_to_all | solution.py:418
  232.9 0.0 copy-done
  232.9 0.1 copy.33
  233.0 0.1 reshape.61
  233.1 0.8 gather_fusion
  233.9 0.0 copy-start.1
  233.9 0.1 reshape.64
  233.9 0.1 copy.34
  234.0 0.1 copy.38
  234.1 0.1 reshape.59
  234.2 0.1 copy.35
  234.3 18.1 %all-to-all-done = f32[128,2,8,128]{3,2,1,0:T(8,128)S(1)} async-done(((f32[128,2,8,128]{3,2,1,0:T(8,128)}), f32[128,2,8,128]{3,2,1,0:T(8,128)S(1)}, u32[]{:S(2)}, u32[]{:S(2)}) %all-to-all-start) | async-done | bytes 1048608 | tf_op jit(solution)/shard_map/all_to_all | solution.py:418
  252.4 0.1 copy.37
  252.5 0.6 gather_fusion.1
  253.1 0.1 broadcast_select_fusion
  253.3 18.0 %all_to_all.10 = f32[16,2,8,8,128]{4,3,2,1,0:T(8,128)S(1)} all-to-all(f32[16,2,8,8,128]{4,3,2,1,0:T(8,128)S(1)} %broadcast_select_fusion), channel_id=1, replica_groups=mesh['ia'=16,'ka'=8] {'ia'}, dimensions={0} | all-to-all | bytes 2097152 | tf_op jit(solution)/shard_map/all_to_all | solution.py:426
  271.3 0.1 copy.39
  271.4 0.3 copy.40
  271.8 0.0 copy-done.1
  271.8 1.1 add_bitcast_fusion
  (4 shorter events, 0.0 us)
Async XLA Ops:
  1.4 231.5 %copy-start = (s32[16,2]{0,1:T(2,128)S(1)}, s32[16,2]{0,1:T(2,128)}, u32[]{:S(2)}) copy-start(s32[16,2]{0,1:T(2,128)} %param.7) | copy-start | bytes 388
  222.4 30.0 %all-to-all-start = ((f32[128,2,8,128]{3,2,1,0:T(8,128)}), f32[128,2,8,128]{3,2,1,0:T(8,128)S(1)}, u32[]{:S(2)}, u32[]{:S(2)}) async-start(f32[128,2,8,128]{3,2,1,0:T(8,128)} %bitcast.4), calls=%async_computation | async-start | bytes 2097152 | tf_op jit(solution)/shard_map/all_to_all | solution.py:418
  233.9 37.9 %copy-start.1 = (f32[2,128,1024]{2,1,0:T(8,128)S(1)}, f32[2,128,1024]{2,1,0:T(8,128)}, u32[]{:S(2)}) copy-start(f32[2,128,1024]{2,1,0:T(8,128)} %get-tuple-element.6) | copy-start | bytes 3145732

commit v3 on v2

--- a/solution.py
+++ b/solution.py
@@ -12,10 +12,10 @@
 STEPS = ((1, 0, 0), (-1, 0, 0), (0, 1, 0), (0, -1, 0), (0, 0, 1), (0, 0, -1))
 HOPS = 32
 LAG = 2
+LATE = HOPS // 2
 SUBS = 2 * HOPS
 CROSS_OWN = 3
 BAND = 256
-CHUNKS = 4
 
 
 def position():
@@ -44,18 +44,24 @@
     return pick(index > HOPS // 2 - 3, index + HOPS // 2, 2 * index + 3)
 
 
-def landing(x, y, z, half, index):
+def yz_rest(y, z, half, index):
     apart = (z - y + SIDE) % SIDE
-    x_way = pick(half == 0, 2 - x, x - 1)
     even = index % 2 == 0
     two_way = pick(half == 0, pick(even, 4, 5), pick(even, 2, 3))
-    way = pick(
-        apart == 0,
-        x_way,
-        pick(apart == 1, pick(half == 0, 4, 3), pick(apart == 3, pick(half == 0, 5, 2), two_way)),
-    )
-    slot = pick(apart == 2, relay_slot(index // 2), index)
-    return way, slot
+    way = pick(apart == 1, pick(half == 0, 4, 3), pick(apart == 3, pick(half == 0, 5, 2), two_way))
+    return way, pick(apart == 2, relay_slot(index // 2), index)
+
+
+def x_rest(x, half, index):
+    return pick(half == 0, 2 - x, x - 1), (index + LATE) % HOPS
+
+
+def landing(x, y, z, half, index):
+    inner = (x == 1) | (x == 2)
+    by_x = inner & ((index < LATE) | (y == z))
+    way, slot = yz_rest(y, z, half, index)
+    x_way, x_slot = x_rest(x, half, index)
+    return pick(by_x, x_way, way), pick(by_x, x_slot, slot)
 
 
 def exchange(t_ref, land, m_buf, arrive, leave, m_sem, swap_arrive, swap_leave):
@@ -104,11 +110,6 @@
             device_id_type=MESH,
         ).start()
 
-    near_y = pick(inner, LAG, 0)
-    near_z = pick(inner, 3 * LAG, 0)
-    far_y = pick(inner, 4, 0)
-    far_z = pick(inner, 4 + 2 * LAG, 0)
-
     relay_from = {2: (5, -1, 4, 4), 3: (4, 5, 5, -1), 4: (3, 2, 2, -1), 5: (2, -1, 3, 3)}
 
     def by_apart(values):
@@ -116,15 +117,7 @@
         return pick(apart == 0, zero, pick(apart == 1, one, pick(apart == 2, two, three)))
 
     def yz_lag(way):
-        along_y = way < 4
-        own, cross = (near_y, far_y) if along_y else (near_z, far_z)
-        through = near_z if along_y else near_y
-        passing = far_z if along_y else far_y
-        values = [through + LAG, passing + LAG, cross, passing + LAG]
-        for place, source in enumerate(relay_from[way]):
-            if source < 0:
-                values[place] = own
-        return by_apart(values)
+        return by_apart([0 if source < 0 or place == 2 else LAG for place, source in enumerate(relay_from[way])])
 
     lags = [
         pick(inner, 0, pick(x == 3, LAG, 2 * LAG)),
@@ -137,8 +130,11 @@
             active = (slot >= 0) & (slot < HOPS)
             if way < 2:
                 half = pick(x == 1 + way, 0, 1)
-                from_t, sub = inner, half * HOPS + slot
-                from_way, from_slot = way, slot
+                index = (slot + LATE) % HOPS
+                from_t = inner & ((slot < LATE) | (apart == 0))
+                sub = half * HOPS + index
+                rest_way, rest_slot = yz_rest(y, z, half, index)
+                from_way, from_slot = pick(inner, rest_way, way), pick(inner, rest_slot, slot)
             else:
                 half = 0 if way < 4 else 1
                 odd = way % 2
@@ -150,12 +146,12 @@
                 places = relay_from[way]
                 near_own = by_apart([places[0] < 0, places[1] < 0, False, places[3] < 0])
                 own = pick(apart == 2, jnp.logical_not(relayed), near_own)
-                from_t = own & jnp.logical_not(inner)
+                from_t = own & (jnp.logical_not(inner) | (index < LATE))
                 sub = half * HOPS + index
-                x_way = (2 - x) if half == 0 else (x - 1)
+                x_way, x_slot = x_rest(x, half, index)
                 relay_way = by_apart([max(place, 0) for place in places])
                 from_way = pick(own, x_way, relay_way)
-                from_slot = pick(own, index, pick(apart == 2, own_slot(relay_index), slot))
+                from_slot = pick(own, x_slot, pick(apart == 2, own_slot(relay_index), slot))
 
             @pl.when(active & from_t)
             def _(way=way, slot=slot, sub=sub):
@@ -168,7 +164,7 @@
 
         return carry
 
-    lax.fori_loop(0, HOPS + 4 + 3 * LAG, step, 0)
+    lax.fori_loop(0, HOPS + 2 * LAG, step, 0)
 
     @pl.when(jnp.logical_not(alone))
     def _():
@@ -204,6 +200,7 @@
     arrive, leave, t_sem, m_sem, w_sem, swap_arrive, swap_leave,
     ring_arrive, ring_leave, relay_arrive, relay_leave, inbox_arrive, inbox_leave,
 ):
+    ring_sems, relay_sems, inbox_sems = (ring_arrive, ring_leave), (relay_arrive, relay_leave), (inbox_arrive, inbox_leave)
     x, y, z, core = position()
     slots, blocks, virtuals = w_buf.shape[0], w_buf.shape[1], w_buf.shape[2]
 
@@ -241,136 +238,161 @@
     lax.fori_loop(0, slots * blocks * tiles, mask_band, 0)
 
     x_half = x // 2
-    part = BAND // CHUNKS
+    half = BAND // 2
+    wide = virtuals // 2
 
     def band_of(s, k):
         return pick(s == 0, y + SIDE - 1 - k, y + 1 + k) % SIDE
 
-    def rows_of(band, chunk):
-        offset = pick(chunk < 2, (1 - x_half) * (BAND // 2), x_half * (BAND // 2) - BAND // 2) + chunk * part
-        return pl.ds(pl.multiple_of(band * BAND + offset, part), part)
-
-    def ring_copy(s, k, chunk):
+    def block_of(s, k, chunk, side):
+        offset = pick(chunk == 0, 1 - x_half, x_half) * half
+        rows = pl.ds(pl.multiple_of(band_of(s, k) * BAND + offset, half), half)
+        return o_buf.at[s, rows, pl.ds(side * wide, wide)]
+
+    def y_beside(s):
+        return device(x, (y + pick(s == 0, 1, SIDE - 1)) % SIDE, z, core)
+
+    def x_beside(s):
+        return device((x + pick(s == 0, 1, SIDE - 1)) % SIDE, y, z, core)
+
+    def remote(source, target, sems, at, where):
         return pltpu.make_async_remote_copy(
-            src_ref=o_buf.at[s, rows_of(band_of(s, k), chunk)],
-            dst_ref=ring.at[s, k, chunk],
-            send_sem=ring_leave.at[s, k, chunk],
-            recv_sem=ring_arrive.at[s, k, chunk],
-            device_id=device(x, (y + pick(s == 0, 1, SIDE - 1)) % SIDE, z, core),
+            src_ref=source,
+            dst_ref=target,
+            send_sem=sems[1].at[at],
+            recv_sem=sems[0].at[at],
+            device_id=where,
             device_id_type=MESH,
         )
 
-    def x_beside(s):
-        return device((x + pick(s == 0, 1, SIDE - 1)) % SIDE, y, z, core)
-
-    def relay_copy(s, chunk):
-        return pltpu.make_async_remote_copy(
-            src_ref=o_buf.at[s, rows_of(y, chunk)],
-            dst_ref=relay.at[s, chunk],
-            send_sem=relay_leave.at[s, chunk],
-            recv_sem=relay_arrive.at[s, chunk],
-            device_id=x_beside(s),
-            device_id_type=MESH,
-        )
-
-    def inbox_copy(s, chunk):
-        return pltpu.make_async_remote_copy(
-            src_ref=relay.at[s, chunk],
-            dst_ref=inbox.at[s, chunk],
-            send_sem=inbox_leave.at[s, chunk],
-            recv_sem=inbox_arrive.at[s, chunk],
-            device_id=x_beside(s),
-            device_id_type=MESH,
-        )
-
-    def absorb(s, k, chunk):
+    def ring_copy(s, k, chunk):
+        return remote(block_of(s, k, chunk, 0), ring.at[s, k, chunk], ring_sems, (s, k, chunk), y_beside(s))
+
+    def last_relay(s):
+        return remote(block_of(s, 3, 0, 0), relay.at[s, SIDE], relay_sems, (s, SIDE), x_beside(s))
+
+    def relay_copy(s, k):
+        return remote(block_of(s, k, 0, 1), relay.at[s, k], relay_sems, (s, k), x_beside(s))
+
+    def pass_on(s, k):
+        relay_copy(s, k).wait_recv()
+        inbox_copy(s, k).start()
+
+    def inbox_copy(s, k):
+        return remote(relay.at[s, k], inbox.at[s, k], inbox_sems, (s, k), x_beside(s))
+
+    def late_copy(s, k):
+        return remote(block_of(s, k, 1, 1), ring.at[s, k, 2], ring_sems, (s, k, 2), y_beside(s))
+
+    def add_left(s, k, chunk):
         ring_copy(s, k - 1, chunk).wait_recv()
-        rows = rows_of(band_of(s, k), chunk)
-        o_buf[s, rows, :] = o_buf[s, rows, :] + ring[s, k - 1, chunk]
+        block = block_of(s, k, chunk, 0)
+        block[...] = block[...] + ring[s, k - 1, chunk]
+
+    def turn_left(s, k, chunk):
+        add_left(s, k, chunk)
+        ring_copy(s, k, chunk).start()
+
+    def turn_right(s, k):
+        inbox_copy(s, k).wait_recv()
+        block = block_of(s, k, 1, 1)
+        if k == 0:
+            block[...] = block[...] + inbox[s, k]
+        else:
+            late_copy(s, k - 1).wait_recv()
+            block[...] = block[...] + inbox[s, k] + ring[s, k - 1, 2]
+        late_copy(s, k).start()
 
     def unit(u, carry):
         s = u % 2
-        band = pl.ds(pl.multiple_of(band_of(s, u // 2) * BAND, BAND), BAND)
+        index = band_of(s, u // 2)
+        band = pl.ds(pl.multiple_of(index * BAND, BAND), BAND)
+        subs = BAND // t_buf.shape[2]
         total = jnp.zeros((2 * BAND, virtuals), jnp.float32)
         for block in range(blocks):
             mirrored = m_buf[block, :, :, band].reshape(virtuals, BAND).T
-            mixed = 2.0 * t_rows(block, u) - mirrored
+            mixed = 2.0 * t_buf[block, pl.ds(index * subs, subs)].reshape(BAND, virtuals) - mirrored
             high = mixed.astype(jnp.bfloat16)
             low = (mixed - high.astype(jnp.float32)).astype(jnp.bfloat16)
             pair = jnp.concatenate([high, low], axis=0)
             total += jnp.dot(pair, w_buf[s, block], preferred_element_type=jnp.float32)
         o_buf[s, band, :] = total[:BAND] + total[BAND:]
+        relay_copy(s, u // 2).start()
 
         @pl.when(u < 2)
         def _():
-            for chunk in range(CHUNKS):
-                ring_copy(s, 0, chunk).start()
-
-        @pl.when((u >= 3) & (u < 3 + CHUNKS))
-        def _():
-            for way in range(2):
-                absorb(way, 1, u - 3)
-                ring_copy(way, 1, u - 3).start()
+            ring_copy(s, 0, 0).start()
+            ring_copy(s, 0, 1).start()
+
+        @pl.when((u == 2) | (u == 3))
+        def _():
+            pass_on(s, 0)
+
+        @pl.when(u == 3)
+        def _():
+            turn_left(0, 1, 0)
+            turn_left(1, 1, 0)
+
+        @pl.when(u == 4)
+        def _():
+            turn_left(0, 1, 1)
+            turn_left(1, 1, 1)
+
+        @pl.when((u == 5) | (u == 6))
+        def _():
+            pass_on(1 - s, 1)
+            turn_right(1 - s, 0)
+
+        @pl.when(u == 6)
+        def _():
+            turn_left(0, 2, 0)
+            turn_left(1, 2, 0)
 
         return carry
 
-    def t_rows(block, u):
-        band = band_of(u % 2, u // 2)
-        subs = BAND // t_buf.shape[2]
-        return t_buf[block, pl.ds(band * subs, subs)].reshape(BAND, virtuals)
-
     lax.fori_loop(0, slots * SIDE, unit, 0)
 
-    def second(chunk, carry):
+    def both(step, *arguments):
         for s in range(2):
-            absorb(s, 2, chunk)
-            ring_copy(s, 2, chunk).start()
-        return carry
-
-    lax.fori_loop(0, CHUNKS, second, 0)
-
-    def third(chunk, carry):
-        for s in range(2):
-            absorb(s, 3, chunk)
-
-        @pl.when(chunk < 2)
-        def _():
-            for s in range(2):
-                relay_copy(s, chunk).start()
-
-        @pl.when(chunk >= 2)
-        def _():
-            for s in range(2):
-                relay_copy(s, chunk - 2).wait_recv()
-                inbox_copy(s, chunk - 2).start()
-
-        return carry
-
-    lax.fori_loop(0, CHUNKS, third, 0)
-
-    for chunk in range(2):
-        for s in range(2):
-            inbox_copy(s, chunk).wait_recv()
-            out_ref[s, pl.ds(chunk * part, part), :] = o_buf[s, rows_of(y, chunk + 2), :] + inbox[s, chunk]
-
-    def drain(chunk, carry):
-        for s in range(2):
-            for k in range(3):
-                ring_copy(s, k, chunk).wait_send()
-        return carry
-
-    lax.fori_loop(0, CHUNKS, drain, 0)
-    for chunk in range(2):
-        for s in range(2):
-            relay_copy(s, chunk).wait_send()
-            inbox_copy(s, chunk).wait_send()
+            step(s, *arguments)
+
+    both(turn_left, 2, 1)
+    both(pass_on, 2)
+    both(turn_right, 1)
+    for s in range(2):
+        add_left(s, 3, 0)
+        last_relay(s).start()
+    both(pass_on, 3)
+    both(turn_right, 2)
+    both(add_left, 3, 1)
+    for s in range(2):
+        last_relay(s).wait_recv()
+        inbox_copy(s, SIDE).start()
+    for s in range(2):
+        inbox_copy(s, 3).wait_recv()
+        late_copy(s, 2).wait_recv()
+        out_ref[s, :, wide:] = block_of(s, 3, 1, 1)[...] + inbox[s, 3] + ring[s, 2, 2]
+    for s in range(2):
+        inbox_copy(s, SIDE).wait_recv()
+        out_ref[s, :, :wide] = block_of(s, 3, 1, 0)[...] + inbox[s, SIDE]
+
+    for s in range(2):
+        for k in range(3):
+            ring_copy(s, k, 0).wait_send()
+            ring_copy(s, k, 1).wait_send()
+            late_copy(s, k).wait_send()
+        for k in range(SIDE):
+            relay_copy(s, k).wait_send()
+            inbox_copy(s, k).wait_send()
+        last_relay(s).wait_send()
+        inbox_copy(s, SIDE).wait_send()
     drain_exchange(land, leave)
 
 
 def summed_rows(amplitudes, integrals, tile_mask):
     slots, blocks, virtuals = integrals.shape[0], integrals.shape[1], integrals.shape[2]
     rows = virtuals // SUBS
-    part = BAND // CHUNKS
+    half, wide = BAND // 2, virtuals // 2
     dma = pltpu.SemaphoreType.DMA
     return pl.pallas_call(
         cycle_kernel,
@@ -385,9 +407,9 @@
             pltpu.VMEM((blocks, SUBS, rows, virtuals), jnp.float32),
             pltpu.VMEM((slots, blocks, virtuals, virtuals), jnp.bfloat16),
             pltpu.VMEM((slots, virtuals, virtuals), jnp.float32),
-            pltpu.VMEM((slots, 3, CHUNKS, part, virtuals), jnp.float32),
-            pltpu.VMEM((slots, 2, part, virtuals), jnp.float32),
-            pltpu.VMEM((slots, 2, part, virtuals), jnp.float32),
+            pltpu.VMEM((slots, 3, 3, half, wide), jnp.float32),
+            pltpu.VMEM((slots, SIDE + 1, half, wide), jnp.float32),
+            pltpu.VMEM((slots, SIDE + 1, half, wide), jnp.float32),
             dma((6, HOPS)),
             dma((6, HOPS)),
             dma,
@@ -395,12 +417,12 @@
             dma,
             dma((2,)),
             dma((2,)),
-            dma((slots, 3, CHUNKS)),
-            dma((slots, 3, CHUNKS)),
-            dma((slots, 2)),
-            dma((slots, 2)),
-            dma((slots, 2)),
-            dma((slots, 2)),
+            dma((slots, 3, 3)),
+            dma((slots, 3, 3)),
+            dma((slots, SIDE + 1)),
+            dma((slots, SIDE + 1)),
+            dma((slots, SIDE + 1)),
+            dma((slots, SIDE + 1)),
         ],
         compiler_params=pltpu.CompilerParams(
             collective_id=0, has_side_effects=True, vmem_limit_bytes=58 << 20

time: 273 us -> 237 us (0.87)
  Pallas kernels: 219 us -> 181 us
    pallas_call x1, Pallas kernels: 219 us -> 181 us  [summed_rows(): pl.pallas_call(cycle_kernel, out_shape=(jax.ShapeDtypeStruct((6, HOPS, bl...]
where the time goes in v3:
time: 237 us
  Pallas kernels  181 us (76%)
  waiting for transfers between devices  18.1 us (8%)
  blocking collectives  18 us (8%)
  starting transfers between devices  12.6 us (5%)
  local copies, waits for them, and re-layouts  6.2 us (3%)
    pallas_call x1, Pallas kernels, summed_rows(): pl.pallas_call(cycle_kernel, out_shape=(jax.ShapeDtypeStruct((6, HOPS, bl...  181 us
    all_to_all x1, waiting for transfers between devices, body(): lax.all_to_all(pieces, ('ia', 'ka'), split_axis=0, concat_axis=0, tiled=T...  18.1 us
    all_to_all x1, blocking collectives, body(): lax.all_to_all(routed, 'ia', split_axis=0, concat_axis=0, tiled=True)  18 us
    all_to_all x1, starting transfers between devices, body(): lax.all_to_all(pieces, ('ia', 'ka'), split_axis=0, concat_axis=0, tiled=T...  12.6 us
  transfers between devices with their start and end apart: 1, of which 1 were waited for; matrix products, arithmetic and copies ran while one was open for 1% of the time, Pallas kernels for 0%

profile of v3, /device:TPU:1, one launch (start us, length us, event | category | flops | bytes accessed | tf_op | source)
XLA Modules:
  0.0 237.2 jit_solution(3426836507312576467)
XLA Ops:
  0.0 1.4 reshape_squeeze.7.mask_ref
  1.4 0.0 copy-start
  1.4 180.9 %shard_map.46 = (f32[6,32,2,16,1024]{4,3,2,1,0:T(8,128)}, f32[2,128,1024]{2,1,0:T(8,128)}) custom-call(f32[2,64,16,1024]{3,2,1,0:T(8,128)} %bitcast.19, bf16[2,2,1024,1024]{3,2,1,0:T(8,128)(2,1)} %bitcast.20, s32[256]{0:T(256)} %reshape_squeeze.7.mask_ref), custom_call_target="tpu_custom_call" | custom-call | tf_op jit(solution)/shard_map/pallas_call | solution.py:397
  182.2 2.3 copy.36
  184.5 12.6 %all-to-all-start = ((f32[128,2,8,128]{3,2,1,0:T(8,128)}), f32[128,2,8,128]{3,2,1,0:T(8,128)S(1)}, u32[]{:S(2)}, u32[]{:S(2)}) async-start(f32[128,2,8,128]{3,2,1,0:T(8,128)} %bitcast.4), calls=%async_computation | async-start | bytes 2097152 | tf_op jit(solution)/shard_map/all_to_all | solution.py:440
  197.2 0.0 copy-done
  197.2 0.1 copy.33
  197.3 0.1 reshape.61
  197.4 0.8 gather_fusion
  198.1 0.0 copy-start.1
  198.1 0.1 reshape.64
  198.2 0.1 copy.34
  198.3 0.1 copy.38
  198.4 0.1 reshape.59
  198.5 0.1 copy.35
  198.6 18.1 %all-to-all-done = f32[128,2,8,128]{3,2,1,0:T(8,128)S(1)} async-done(((f32[128,2,8,128]{3,2,1,0:T(8,128)}), f32[128,2,8,128]{3,2,1,0:T(8,128)S(1)}, u32[]{:S(2)}, u32[]{:S(2)}) %all-to-all-start) | async-done | bytes 1048608 | tf_op jit(solution)/shard_map/all_to_all | solution.py:440
  216.7 0.1 copy.37
  216.8 0.6 gather_fusion.1
  217.4 0.1 broadcast_select_fusion
  217.6 18.0 %all_to_all.10 = f32[16,2,8,8,128]{4,3,2,1,0:T(8,128)S(1)} all-to-all(f32[16,2,8,8,128]{4,3,2,1,0:T(8,128)S(1)} %broadcast_select_fusion), channel_id=1, replica_groups=mesh['ia'=16,'ka'=8] {'ia'}, dimensions={0} | all-to-all | bytes 2097152 | tf_op jit(solution)/shard_map/all_to_all | solution.py:448
  235.6 0.1 copy.39
  235.7 0.3 copy.40
  236.0 0.0 copy-done.1
  236.0 1.1 add_bitcast_fusion
  (4 shorter events, 0.0 us)
Async XLA Ops:
  1.4 195.8 %copy-start = (s32[16,2]{0,1:T(2,128)S(1)}, s32[16,2]{0,1:T(2,128)}, u32[]{:S(2)}) copy-start(s32[16,2]{0,1:T(2,128)} %param.7) | copy-start | bytes 388
  184.5 32.1 %all-to-all-start = ((f32[128,2,8,128]{3,2,1,0:T(8,128)}), f32[128,2,8,128]{3,2,1,0:T(8,128)S(1)}, u32[]{:S(2)}, u32[]{:S(2)}) async-start(f32[128,2,8,128]{3,2,1,0:T(8,128)} %bitcast.4), calls=%async_computation | async-start | bytes 2097152 | tf_op jit(solution)/shard_map/all_to_all | solution.py:440
  198.1 37.9 %copy-start.1 = (f32[2,128,1024]{2,1,0:T(8,128)S(1)}, f32[2,128,1024]{2,1,0:T(8,128)}, u32[]{:S(2)}) copy-start(f32[2,128,1024]{2,1,0:T(8,128)} %get-tuple-element.6) | copy-start | bytes 3145732

commit v4 on v3

--- a/solution.py
+++ b/solution.py
@@ -12,6 +12,7 @@
 STEPS = ((1, 0, 0), (-1, 0, 0), (0, 1, 0), (0, -1, 0), (0, 0, 1), (0, 0, -1))
 HOPS = 32
 LAG = 2
+MASK_FROM = 4
 LATE = HOPS // 2
 SUBS = 2 * HOPS
 CROSS_OWN = 3
@@ -64,7 +65,7 @@
     return pick(by_x, x_way, way), pick(by_x, x_slot, slot)
 
 
-def exchange(t_ref, land, m_buf, arrive, leave, m_sem, swap_arrive, swap_leave):
+def exchange(t_ref, land, m_buf, arrive, leave, m_sem, swap_arrive, swap_leave, work):
     x, y, z, core = position()
     inner = (x == 1) | (x == 2)
     apart = (z - y + SIDE) % SIDE
@@ -162,6 +163,7 @@
                 landed(from_way, from_slot)
                 send_on(way, slot, from_way, from_slot)
 
+        work(t)
         return carry
 
     lax.fori_loop(0, HOPS + 2 * LAG, step, 0)
@@ -195,47 +197,60 @@
 
 
 def cycle_kernel(
-    t_ref, w_ref, mask_ref, land, out_ref,
+    t_ref, w_ref, mask_ref, land, out_ref, spread,
     t_buf, m_buf, w_buf, o_buf, ring, relay, inbox,
     arrive, leave, t_sem, m_sem, w_sem, swap_arrive, swap_leave,
     ring_arrive, ring_leave, relay_arrive, relay_leave, inbox_arrive, inbox_leave,
+    spread_arrive, spread_leave,
 ):
     ring_sems, relay_sems, inbox_sems = (ring_arrive, ring_leave), (relay_arrive, relay_leave), (inbox_arrive, inbox_leave)
     x, y, z, core = position()
     slots, blocks, virtuals = w_buf.shape[0], w_buf.shape[1], w_buf.shape[2]
 
+    row_groups, col_groups = lax.axis_size("ia"), lax.axis_size("ka")
+    devices = row_groups * col_groups
+    row, col = lax.axis_index("ia"), lax.axis_index("ka")
     barrier = pltpu.get_barrier_semaphore()
-    for way in range(6):
-        for other in range(2):
-            pl.semaphore_signal(
-                barrier, inc=1, device_id=device(*towards(x, y, z, way), other), device_id_type=MESH
-            )
-    pl.semaphore_signal(barrier, inc=1, device_id=device(x, y, z, 1 - core), device_id_type=MESH)
-    pl.semaphore_wait(barrier, 13)
+
+    def greet(n, carry):
+        other = (row * col_groups + col + n) % devices
+        pl.semaphore_signal(
+            barrier, inc=1, device_id=(other // col_groups, other % col_groups), device_id_type=MESH
+        )
+        return carry
+
+    lax.fori_loop(1, devices, greet, 0)
+    pl.semaphore_wait(barrier, devices - 1)
 
     load_t = pltpu.make_async_copy(t_ref, t_buf, t_sem)
     load_w = pltpu.make_async_copy(w_ref, w_buf, w_sem)
     load_t.start()
     load_w.start()
 
-    exchange(t_ref, land, m_buf, arrive, leave, m_sem, swap_arrive, swap_leave)
-
-    load_t.wait()
-    load_w.wait()
     tiles = 8
     tile = virtuals // tiles
 
-    def mask_band(n, carry):
+    def mask_band(n):
         s, block, r = n // (blocks * tiles), (n // tiles) % blocks, n % tiles
         band = pl.ds(pl.multiple_of(r * tile, tile), tile)
         for c in range(tiles):
-            keep = mask_ref[n * tiles + c]
+            keep = mask_ref[s, block, r, c]
             columns = pl.ds(c * tile, tile)
             value = w_buf[s, block, band, columns]
             w_buf[s, block, band, columns] = jnp.where(keep != 0, value, jnp.zeros_like(value))
-        return carry
-
-    lax.fori_loop(0, slots * blocks * tiles, mask_band, 0)
+
+    def work(t):
+        @pl.when(t == MASK_FROM)
+        def _():
+            load_t.wait()
+            load_w.wait()
+
+        @pl.when((t >= MASK_FROM) & (t < MASK_FROM + slots * blocks * tiles // 2))
+        def _():
+            mask_band(2 * (t - MASK_FROM))
+            mask_band(2 * (t - MASK_FROM) + 1)
+
+    exchange(t_ref, land, m_buf, arrive, leave, m_sem, swap_arrive, swap_leave, work)
 
     x_half = x // 2
     half = BAND // 2
@@ -368,13 +383,49 @@
     for s in range(2):
         last_relay(s).wait_recv()
         inbox_copy(s, SIDE).start()
+    thin, slim = half // row_groups, virtuals // col_groups
+
+    def piece_of(to_row, to_col):
+        rows = pl.ds(pl.multiple_of(to_row * thin, thin), thin)
+        columns = pl.ds(pl.multiple_of(to_col * slim, slim), slim)
+        return out_ref.at[:, rows, columns]
+
+    def scatter(side):
+        span = col_groups // 2
+
+        def send(n, carry):
+            to_row = (row + n // span) % row_groups
+            to_col = side * span + (col + n) % span
+            target = spread.at[row * col_groups + col]
+
+            @pl.when((to_row == row) & (to_col == col))
+            def _():
+                pltpu.make_async_copy(piece_of(to_row, to_col), target, spread_arrive).start()
+
+            @pl.when((to_row != row) | (to_col != col))
+            def _():
+                pltpu.make_async_remote_copy(
+                    src_ref=piece_of(to_row, to_col),
+                    dst_ref=target,
+                    send_sem=spread_leave,
+                    recv_sem=spread_arrive,
+                    device_id=(to_row, to_col),
+                    device_id_type=MESH,
+                ).start()
+
+            return carry
+
+        lax.fori_loop(0, row_groups * span, send, 0)
+
     for s in range(2):
         inbox_copy(s, 3).wait_recv()
         late_copy(s, 2).wait_recv()
         out_ref[s, :, wide:] = block_of(s, 3, 1, 1)[...] + inbox[s, 3] + ring[s, 2, 2]
+    scatter(1)
     for s in range(2):
         inbox_copy(s, SIDE).wait_recv()
         out_ref[s, :, :wide] = block_of(s, 3, 1, 0)[...] + inbox[s, SIDE]
+    scatter(0)
 
     for s in range(2):
         for k in range(3):
@@ -387,6 +438,9 @@
         last_relay(s).wait_send()
         inbox_copy(s, SIDE).wait_send()
     drain_exchange(land, leave)
+    sent = spread.at[pl.ds(0, devices - 1)]
+    pltpu.make_async_copy(sent, sent, spread_leave).wait()
+    pltpu.make_async_copy(spread, spread, spread_arrive).wait()
 
 
 def summed_rows(amplitudes, integrals, tile_mask):
@@ -394,14 +448,17 @@
     rows = virtuals // SUBS
     half, wide = BAND // 2, virtuals // 2
     dma = pltpu.SemaphoreType.DMA
+    row_groups, col_groups = lax.axis_size("ia"), lax.axis_size("ka")
+    devices = row_groups * col_groups
     return pl.pallas_call(
         cycle_kernel,
         out_shape=(
             jax.ShapeDtypeStruct((6, HOPS, blocks, rows, virtuals), jnp.float32),
-            jax.ShapeDtypeStruct((slots, BAND // 2, virtuals), jnp.float32),
+            jax.ShapeDtypeStruct((slots, half, virtuals), jnp.float32),
+            jax.ShapeDtypeStruct((devices, slots, half // row_groups, virtuals // col_groups), jnp.float32),
         ),
         in_specs=[HBM, HBM, pl.BlockSpec(memory_space=pltpu.SMEM)],
-        out_specs=(HBM, pl.BlockSpec(memory_space=pltpu.VMEM)),
+        out_specs=(HBM, pl.BlockSpec(memory_space=pltpu.VMEM), HBM),
         scratch_shapes=[
             pltpu.VMEM((blocks, SUBS, rows, virtuals), jnp.float32),
             pltpu.VMEM((blocks, SUBS, rows, virtuals), jnp.float32),
@@ -423,21 +480,20 @@
             dma((slots, SIDE + 1)),
             dma((slots, SIDE + 1)),
             dma((slots, SIDE + 1)),
+            dma,
+            dma,
         ],
         compiler_params=pltpu.CompilerParams(
             collective_id=0, has_side_effects=True, vmem_limit_bytes=58 << 20
         ),
-    )(amplitudes.reshape(blocks, SUBS, rows, virtuals), integrals, tile_mask.reshape(-1))[1]
+    )(amplitudes.reshape(blocks, SUBS, rows, virtuals), integrals, tile_mask)[1:]
 
 
 def body(amplitudes, integrals, tile_mask, pair_list):
-    own_rows = summed_rows(amplitudes[0], integrals[0], tile_mask[0])
+    own_rows, spread = summed_rows(amplitudes[0], integrals[0], tile_mask[0])
     row_groups, col_groups = lax.axis_size("ia"), lax.axis_size("ka")
     slots, rows, virtuals = own_rows.shape
     thin, wide = rows // row_groups, virtuals // col_groups
-    pieces = own_rows.reshape(slots, row_groups, thin, col_groups, wide).transpose(1, 3, 0, 2, 4)
-    pieces = pieces.reshape(row_groups * col_groups, slots, thin, wide)
-    spread = lax.all_to_all(pieces, ("ia", "ka"), split_axis=0, concat_axis=0, tiled=True)
     spread = spread.reshape(row_groups, col_groups, slots, thin, wide).transpose(0, 2, 1, 3, 4)
     spread = spread.reshape(row_groups * slots, col_groups, thin, wide)
     owners = jnp.arange(row_groups, dtype=jnp.int32)

time: 237 us -> 228 us (0.962)
  Pallas kernels: 181 us -> 202 us
  waiting for transfers between devices: 18.1 us -> 0 us
  starting transfers between devices: 12.6 us -> 0 us
  blocking collectives: 18 us -> 20.6 us
  local copies, waits for them, and re-layouts: 6.2 us -> 3.76 us
    pallas_call x1, Pallas kernels: 181 us -> 202 us  [summed_rows(): pl.pallas_call(cycle_kernel, out_shape=(jax.ShapeDtypeStruct((6, HOPS, bl...]
    all_to_all x1 -> x0, waiting for transfers between devices: 18.1 us -> none  [body(): lax.all_to_all(pieces, ('ia', 'ka'), split_axis=0, concat_axis=0, tiled=T...]
    all_to_all x1 -> x0, starting transfers between devices: 12.6 us -> none  [body(): lax.all_to_all(pieces, ('ia', 'ka'), split_axis=0, concat_axis=0, tiled=T...]
    all_to_all x1, blocking collectives: 18 us -> 20.6 us  [body(): lax.all_to_all(routed, 'ia', split_axis=0, concat_axis=0, tiled=True)]
    transpose x2 -> x0, local copies, waits for them, and re-layouts: 2.4 us -> none  [the longest x1 2.29 us: body(): own_rows.reshape(slots, row_groups, thin, col_groups, wide)]
  transfers between devices with their start and end apart: 1 -> 0, of which waited for: 1 -> 0; matrix products, arithmetic and copies ran while one was open for 1% -> 0% of each run, Pallas kernels for 0% -> 0%
where the time goes in v4:
time: 228 us; the launch traced here: 227 us
  Pallas kernels  202 us (89%)
  blocking collectives  20.6 us (9%)
  local copies, waits for them, and re-layouts  3.76 us (2%)
    pallas_call x1, Pallas kernels, summed_rows(): pl.pallas_call(cycle_kernel, out_shape=(jax.ShapeDtypeStruct((6, HOPS, bl...  202 us
    all_to_all x1, blocking collectives, body(): lax.all_to_all(routed, 'ia', split_axis=0, concat_axis=0, tiled=True)  20.6 us

profile of v4, /device:TPU:1, one launch (start us, length us, event | category | flops | bytes accessed | tf_op | source)
XLA Modules:
  0.0 227.3 jit_solution(10120925024644205399)
XLA Ops:
  0.0 0.0 copy-start
  0.0 201.6 %shard_map.46 = (f32[6,32,2,16,1024]{4,3,2,1,0:T(8,128)}, f32[2,128,1024]{2,1,0:T(8,128)}, f32[128,2,8,128]{3,2,1,0:T(8,128)}) custom-call(f32[2,64,16,1024]{3,2,1,0:T(8,128)} %bitcast.14, bf16[2,2,1024,1024]{3,2,1,0:T(8,128)(2,1)} %bitcast.15, s32[2,2,8,8]{3,2,1,0:T(8,128)} %bitcast.21), custom_call_target="tpu_custom_call" | custom-call | tf_op jit(solution)/shard_map/pallas_call | solution.py:453
  201.6 1.3 copy.26
  202.9 0.0 copy-done
  202.9 0.1 copy.23
  203.0 0.1 reshape.53
  203.1 0.0 copy-start.1
  203.1 0.8 gather_fusion
  203.9 0.1 reshape.56
  204.0 0.1 copy.24
  204.1 0.1 copy.27
  204.2 0.1 reshape.51
  204.3 0.1 copy.25
  204.4 0.6 gather_fusion.1
  205.0 0.1 broadcast_select_fusion
  205.1 20.6 %all_to_all.5 = f32[16,2,8,8,128]{4,3,2,1,0:T(8,128)S(1)} all-to-all(f32[16,2,8,8,128]{4,3,2,1,0:T(8,128)S(1)} %broadcast_select_fusion), channel_id=1, replica_groups=mesh['ia'=16,'ka'=8] {'ia'}, dimensions={0} | all-to-all | bytes 2097152 | tf_op jit(solution)/shard_map/all_to_all | solution.py:504
  225.7 0.1 copy.28
  225.8 0.3 copy.29
  226.2 0.0 copy-done.1
  226.2 1.1 add_bitcast_fusion
  (4 shorter events, 0.0 us)
Async XLA Ops:
  0.0 202.9 %copy-start = (s32[16,2]{0,1:T(2,128)S(1)}, s32[16,2]{0,1:T(2,128)}, u32[]{:S(2)}) copy-start(s32[16,2]{0,1:T(2,128)} %param.7) | copy-start | bytes 388
  203.1 23.1 %copy-start.1 = (f32[2,128,1024]{2,1,0:T(8,128)S(1)}, f32[2,128,1024]{2,1,0:T(8,128)}, u32[]{:S(2)}) copy-start(f32[2,128,1024]{2,1,0:T(8,128)} %get-tuple-element.7) | copy-start | bytes 3145732

commit v5 on v4

--- a/solution.py
+++ b/solution.py
@@ -197,11 +197,11 @@
 
 
 def cycle_kernel(
-    t_ref, w_ref, mask_ref, land, out_ref, spread,
+    t_ref, w_ref, mask_ref, pair_ref, land, out_ref,
     t_buf, m_buf, w_buf, o_buf, ring, relay, inbox,
     arrive, leave, t_sem, m_sem, w_sem, swap_arrive, swap_leave,
     ring_arrive, ring_leave, relay_arrive, relay_leave, inbox_arrive, inbox_leave,
-    spread_arrive, spread_leave,
+    own, spread, stage, final, spread_arrive, spread_leave, final_arrive, final_leave,
 ):
     ring_sems, relay_sems, inbox_sems = (ring_arrive, ring_leave), (relay_arrive, relay_leave), (inbox_arrive, inbox_leave)
     x, y, z, core = position()
@@ -388,7 +388,7 @@
     def piece_of(to_row, to_col):
         rows = pl.ds(pl.multiple_of(to_row * thin, thin), thin)
         columns = pl.ds(pl.multiple_of(to_col * slim, slim), slim)
-        return out_ref.at[:, rows, columns]
+        return own.at[:, rows, columns]
 
     def scatter(side):
         span = col_groups // 2
@@ -420,12 +420,38 @@
     for s in range(2):
         inbox_copy(s, 3).wait_recv()
         late_copy(s, 2).wait_recv()
-        out_ref[s, :, wide:] = block_of(s, 3, 1, 1)[...] + inbox[s, 3] + ring[s, 2, 2]
+        own[s, :, wide:] = block_of(s, 3, 1, 1)[...] + inbox[s, 3] + ring[s, 2, 2]
     scatter(1)
     for s in range(2):
         inbox_copy(s, SIDE).wait_recv()
-        out_ref[s, :, :wide] = block_of(s, 3, 1, 0)[...] + inbox[s, SIDE]
+        own[s, :, :wide] = block_of(s, 3, 1, 0)[...] + inbox[s, SIDE]
     scatter(0)
+    pltpu.make_async_copy(spread, spread, spread_arrive).wait()
+
+    def route(i, carry):
+        for s in range(slots):
+            j = pair_ref[s, i]
+            t = jnp.where(pair_ref[0, j] == i, 0, 1)
+            for k in range(col_groups):
+                stage[i, s, k] = spread[j * col_groups + k, t]
+        return carry
+
+    lax.fori_loop(0, row_groups, route, 0)
+    pltpu.make_async_copy(stage.at[row], final.at[row], final_arrive).start()
+
+    def deliver(n, carry):
+        to_row = (row + n) % row_groups
+        pltpu.make_async_remote_copy(
+            src_ref=stage.at[to_row],
+            dst_ref=final.at[row],
+            send_sem=final_leave,
+            recv_sem=final_arrive,
+            device_id=(to_row, col),
+            device_id_type=MESH,
+        ).start()
+        return carry
+
+    lax.fori_loop(1, row_groups, deliver, 0)
 
     for s in range(2):
         for k in range(3):
@@ -440,25 +466,32 @@
     drain_exchange(land, leave)
     sent = spread.at[pl.ds(0, devices - 1)]
     pltpu.make_async_copy(sent, sent, spread_leave).wait()
-    pltpu.make_async_copy(spread, spread, spread_arrive).wait()
-
-
-def summed_rows(amplitudes, integrals, tile_mask):
+
+    pltpu.make_async_copy(final, final, final_arrive).wait()
+    for s in range(slots):
+        for k in range(col_groups):
+            columns = pl.ds(k * half, half)
+            out_ref[s, :, columns] = own[s, :, columns] + final[:, s, k].reshape(half, slim).T
+    delivered = final.at[pl.ds(0, row_groups - 1)]
+    pltpu.make_async_copy(delivered, delivered, final_leave).wait()
+
+
+def residual_rows(amplitudes, integrals, tile_mask, pair_list):
     slots, blocks, virtuals = integrals.shape[0], integrals.shape[1], integrals.shape[2]
     rows = virtuals // SUBS
     half, wide = BAND // 2, virtuals // 2
     dma = pltpu.SemaphoreType.DMA
     row_groups, col_groups = lax.axis_size("ia"), lax.axis_size("ka")
     devices = row_groups * col_groups
+    thin, slim = half // row_groups, virtuals // col_groups
     return pl.pallas_call(
         cycle_kernel,
         out_shape=(
             jax.ShapeDtypeStruct((6, HOPS, blocks, rows, virtuals), jnp.float32),
             jax.ShapeDtypeStruct((slots, half, virtuals), jnp.float32),
-            jax.ShapeDtypeStruct((devices, slots, half // row_groups, virtuals // col_groups), jnp.float32),
         ),
-        in_specs=[HBM, HBM, pl.BlockSpec(memory_space=pltpu.SMEM)],
-        out_specs=(HBM, pl.BlockSpec(memory_space=pltpu.VMEM), HBM),
+        in_specs=[HBM, HBM, pl.BlockSpec(memory_space=pltpu.SMEM), pl.BlockSpec(memory_space=pltpu.SMEM)],
+        out_specs=(HBM, pl.BlockSpec(memory_space=pltpu.VMEM)),
         scratch_shapes=[
             pltpu.VMEM((blocks, SUBS, rows, virtuals), jnp.float32),
             pltpu.VMEM((blocks, SUBS, rows, virtuals), jnp.float32),
@@ -480,30 +513,23 @@
             dma((slots, SIDE + 1)),
             dma((slots, SIDE + 1)),
             dma((slots, SIDE + 1)),
+            pltpu.VMEM((slots, half, virtuals), jnp.float32),
+            pltpu.VMEM((devices, slots, thin, slim), jnp.float32),
+            pltpu.VMEM((row_groups, slots, col_groups, thin, slim), jnp.float32),
+            pltpu.VMEM((row_groups, slots, col_groups, thin, slim), jnp.float32),
+            dma,
+            dma,
             dma,
             dma,
         ],
         compiler_params=pltpu.CompilerParams(
             collective_id=0, has_side_effects=True, vmem_limit_bytes=58 << 20
         ),
-    )(amplitudes.reshape(blocks, SUBS, rows, virtuals), integrals, tile_mask)[1:]
+    )(amplitudes.reshape(blocks, SUBS, rows, virtuals), integrals, tile_mask, pair_list)[1]
 
 
 def body(amplitudes, integrals, tile_mask, pair_list):
-    own_rows, spread = summed_rows(amplitudes[0], integrals[0], tile_mask[0])
-    row_groups, col_groups = lax.axis_size("ia"), lax.axis_size("ka")
-    slots, rows, virtuals = own_rows.shape
-    thin, wide = rows // row_groups, virtuals // col_groups
-    spread = spread.reshape(row_groups, col_groups, slots, thin, wide).transpose(0, 2, 1, 3, 4)
-    spread = spread.reshape(row_groups * slots, col_groups, thin, wide)
-    owners = jnp.arange(row_groups, dtype=jnp.int32)
-    partner_slot = jnp.where(pair_list[pair_list, 0] == owners[:, None], 0, 1).astype(jnp.int32)
-    source_row = pair_list * 2 + partner_slot
-    routed = jnp.take(spread, source_row.reshape(-1), axis=0)
-    routed = routed.reshape(row_groups, slots, col_groups, thin, wide)
-    delivered = lax.all_to_all(routed, "ia", split_axis=0, concat_axis=0, tiled=True)
-    mirrored = delivered.transpose(1, 4, 2, 0, 3).reshape(slots, wide, virtuals)
-    return (own_rows + mirrored)[None]
+    return residual_rows(amplitudes[0], integrals[0], tile_mask[0], pair_list.T)[None]
 
 
 def solution(mesh):

time: 228 us -> 220 us (0.965)
  blocking collectives: 20.6 us -> 0 us
  Pallas kernels: 202 us -> 217 us
    all_to_all x1 -> x0, blocking collectives: 20.6 us -> none  [body(): lax.all_to_all(routed, 'ia', split_axis=0, concat_axis=0, tiled=True)]
    pallas_call x1, Pallas kernels: 202 us -> 217 us  [residual_rows(): pl.pallas_call(cycle_kernel, out_shape=(jax.ShapeDtypeStruct((6, HOPS, bl...]
    unnamed x4 -> x1, local copies, waits for them, and re-layouts: 0.01 us -> 2.31 us
where the time goes in v5:
time: 220 us; the launch traced here: 219 us
  Pallas kernels  217 us (99%)
  local copies, waits for them, and re-layouts  2.31 us (1%)
    pallas_call x1, Pallas kernels, residual_rows(): pl.pallas_call(cycle_kernel, out_shape=(jax.ShapeDtypeStruct((6, HOPS, bl...  217 us

profile of v5, /device:TPU:1, one launch (start us, length us, event | category | flops | bytes accessed | tf_op | source)
XLA Modules:
  0.0 219.4 jit_solution(5075267542522564954)
XLA Ops:
  0.0 217.1 %shard_map.46 = (f32[6,32,2,16,1024]{4,3,2,1,0:T(8,128)}, f32[2,128,1024]{2,1,0:T(8,128)}) custom-call(f32[2,64,16,1024]{3,2,1,0:T(8,128)} %bitcast.5, bf16[2,2,1024,1024]{3,2,1,0:T(8,128)(2,1)} %bitcast.6, s32[2,2,8,8]{3,2,1,0:T(8,128)} %bitcast.8, s32[2,16]{1,0:T(2,128)} %bitcast.9), custom_call_target="tpu_custom_call" | custom-call | tf_op jit(solution)/shard_map/pallas_call | solution.py:487
  217.1 2.3 %copy.6 = f32[1,2,128,1024]{3,2,1,0:T(8,128)} copy(f32[1,2,128,1024]{3,2,1,0:T(8,128)} %bitcast.7) | data formatting | bytes 2097152

commit v6 on v5

--- a/solution.py
+++ b/solution.py
@@ -488,7 +488,7 @@
         cycle_kernel,
         out_shape=(
             jax.ShapeDtypeStruct((6, HOPS, blocks, rows, virtuals), jnp.float32),
-            jax.ShapeDtypeStruct((slots, half, virtuals), jnp.float32),
+            pltpu.VMEM((slots, half, virtuals), jnp.float32),
         ),
         in_specs=[HBM, HBM, pl.BlockSpec(memory_space=pltpu.SMEM), pl.BlockSpec(memory_space=pltpu.SMEM)],
         out_specs=(HBM, pl.BlockSpec(memory_space=pltpu.VMEM)),

time: 220 us -> 218 us (level)
  no operation moved by 1% of the time
where the time goes in v6:
time: 218 us; the launch traced here: 217 us
  Pallas kernels  216 us (99%)
    pallas_call x1, Pallas kernels, residual_rows(): pl.pallas_call(cycle_kernel, out_shape=(jax.ShapeDtypeStruct((6, HOPS, bl...  216 us

profile of v6, /device:TPU:1, one launch (start us, length us, event | category | flops | bytes accessed | tf_op | source)
XLA Modules:
  0.0 217.0 jit_solution(18037416664313865694)
XLA Ops:
  0.0 216.0 %shard_map.46 = (f32[6,32,2,16,1024]{4,3,2,1,0:T(8,128)}, f32[2,128,1024]{2,1,0:T(8,128)S(1)}) custom-call(f32[2,64,16,1024]{3,2,1,0:T(8,128)} %bitcast.6, bf16[2,2,1024,1024]{3,2,1,0:T(8,128)(2,1)} %bitcast.7, s32[2,2,8,8]{3,2,1,0:T(8,128)} %bitcast.8, s32[2,16]{1,0:T(2,128)} %bitcast.9), custom_call_target="tpu_custom_call" | custom-call | tf_op jit(solution)/shard_map/pallas_call | solution.py:487
  216.0 1.0 copy.6

commit v7 on v6

--- a/solution.py
+++ b/solution.py
@@ -212,14 +212,17 @@
     row, col = lax.axis_index("ia"), lax.axis_index("ka")
     barrier = pltpu.get_barrier_semaphore()
 
-    def greet(n, carry):
-        other = (row * col_groups + col + n) % devices
-        pl.semaphore_signal(
-            barrier, inc=1, device_id=(other // col_groups, other % col_groups), device_id_type=MESH
-        )
+    def greet(to_row, to_col):
+        pl.semaphore_signal(barrier, inc=1, device_id=(to_row, to_col), device_id_type=MESH)
+
+    def greet_row(n, carry):
+        for to_col in range(col_groups):
+            greet((row + n) % row_groups, to_col)
         return carry
 
-    lax.fori_loop(1, devices, greet, 0)
+    lax.fori_loop(1, row_groups, greet_row, 0)
+    for turn in range(1, col_groups):
+        greet(row, (col + turn) % col_groups)
     pl.semaphore_wait(barrier, devices - 1)
 
     load_t = pltpu.make_async_copy(t_ref, t_buf, t_sem)

time: 218 us -> 216 us (level)
    pallas_call x1, Pallas kernels: 216 us -> 214 us  [residual_rows(): pl.pallas_call(cycle_kernel, out_shape=(jax.ShapeDtypeStruct((6, HOPS, bl...]
where the time goes in v7:
time: 216 us; the launch traced here: 215 us
  Pallas kernels  214 us (99%)
    pallas_call x1, Pallas kernels, residual_rows(): pl.pallas_call(cycle_kernel, out_shape=(jax.ShapeDtypeStruct((6, HOPS, bl...  214 us

profile of v7, /device:TPU:1, one launch (start us, length us, event | category | flops | bytes accessed | tf_op | source)
XLA Modules:
  0.0 214.5 jit_solution(4921769071155612403)
XLA Ops:
  0.0 213.6 %shard_map.46 = (f32[6,32,2,16,1024]{4,3,2,1,0:T(8,128)}, f32[2,128,1024]{2,1,0:T(8,128)S(1)}) custom-call(f32[2,64,16,1024]{3,2,1,0:T(8,128)} %bitcast.6, bf16[2,2,1024,1024]{3,2,1,0:T(8,128)(2,1)} %bitcast.7, s32[2,2,8,8]{3,2,1,0:T(8,128)} %bitcast.8, s32[2,16]{1,0:T(2,128)} %bitcast.9), custom_call_target="tpu_custom_call" | custom-call | tf_op jit(solution)/shard_map/pallas_call | solution.py:490
  213.6 1.0 copy.6
